TPU v7x, 1024 devices: a whole 4x8x16 slice. The times are simulated.
1024 devices in a mesh: shard: 64 (over y_lo, z), rep: 16 (over x, y_hi, core).
Axes of the slice: x: 4, y: 8 (y_hi: 2, y_lo: 4; y = y_hi * 4 + y_lo), z: 16, core: 2. Of those that a mesh axis runs over, the one named last changes fastest.
Arguments:
- images: bfloat16 [1024, 8, 16, 768], P(('shard', 'rep')), may hold values from -24 to 24
- cotangent: bfloat16 [1024, 8, 16, 1536], P(('shard', 'rep')), may hold values from -6 to 6
- depthwise_weight: bfloat16 [768, 49], P('shard'), may hold values from -0.875 to 0.875
- norm_gain: bfloat16 [768], P('shard'), may hold values from 0.5 to 1.5
- norm_bias: bfloat16 [768], P('shard'), may hold values from -3 to 3
- up_weight: bfloat16 [768, 1536], P('shard'), may hold values from -0.21875 to 0.21875
Outputs:
- grad_images: bfloat16 [1024, 8, 16, 768], P(('shard', 'rep'))
- grad_up: float32 [768, 1536], P('shard')
- grad_depthwise: float32 [768, 49], P('shard')
- grad_gain: float32 [768], P('shard')
- grad_bias: float32 [768], P('shard')
All inputs are finite; a program needn't handle non-finite values.
Results may differ from a plain program's by a relative error of at most 0.0056.
Values may be sent and summed in bfloat16 or wider, within the bound.
A program may use at most 128 MiB of HBM per device.

v0:
```python
import math

import jax
import jax.numpy as jnp
from jax import lax
from jax.sharding import PartitionSpec as P

KS = 7


norm_eps = 1e-06


def gelu_slope(inputs):
    cumulative = 0.5 * (1.0 + lax.erf(inputs * 0.7071067811865476))
    return cumulative + inputs * jnp.exp(-0.5 * inputs * inputs) * 0.3989422804014327


def pad_tile(source, margin):
    return jnp.pad(source, ((0, 0), (margin, margin), (margin, margin), (0, 0)))


def depthwise(source, kernel, extent):
    margin = extent // 2
    height, breadth = (source.shape[1], source.shape[2])
    padded = pad_tile(source, margin)
    running = jnp.zeros_like(source)
    for down_step in range(extent):
        for across in range(extent):
            running = (
                running
                + padded[:, down_step : down_step + height, across : across + breadth, :]
                * kernel[:, down_step * extent + across]
            )
    return running


def depthwise_back(grad_conv, kernel, extent):
    margin = extent // 2
    height, breadth = (grad_conv.shape[1], grad_conv.shape[2])
    padded = pad_tile(grad_conv, margin)
    running = jnp.zeros_like(grad_conv)
    for down_step in range(extent):
        for across in range(extent):
            top = 2 * margin - down_step
            left = 2 * margin - across
            running = (
                running
                + padded[:, top : top + height, left : left + breadth, :]
                * kernel[:, down_step * extent + across]
            )
    return running


def kernel_grad(source, grad_conv, extent):
    margin = extent // 2
    height, breadth = (source.shape[1], source.shape[2])
    padded = pad_tile(source, margin)
    columns = []
    for down_step in range(extent):
        for across in range(extent):
            columns.append(
                jnp.sum(
                    grad_conv
                    * padded[:, down_step : down_step + height, across : across + breadth, :],
                    axis=(0, 1, 2),
                )
            )
    return jnp.stack(columns, axis=1)


def local_pass(x_tile, cot_tile, dw_weight, gain, bias, weight, extent):
    source = x_tile.astype(jnp.float32)
    kernel = dw_weight.astype(jnp.float32)
    conv_out = depthwise(source, kernel, extent)
    average = jnp.mean(conv_out, axis=-1, keepdims=True)
    centered = conv_out - average
    inv_std = lax.rsqrt(jnp.mean(centered * centered, axis=-1, keepdims=True) + norm_eps)
    whitened = centered * inv_std
    gain_f = gain.astype(jnp.float32)
    normed = (whitened * gain_f + bias.astype(jnp.float32)).astype(jnp.bfloat16)
    depth = source.shape[-1]
    hidden = weight.shape[1]
    flattened = normed.reshape(-1, depth)
    pre_act = jnp.dot(flattened, weight, preferred_element_type=jnp.float32)
    grad_pre = (cot_tile.reshape(-1, hidden).astype(jnp.float32) * gelu_slope(pre_act)).astype(
        jnp.bfloat16
    )
    grad_normed = lax.dot_general(
        grad_pre, weight, (((1,), (1,)), ((), ())), preferred_element_type=jnp.float32
    ).reshape(conv_out.shape)
    weight_term = lax.dot_general(
        flattened, grad_pre, (((0,), (0,)), ((), ())), preferred_element_type=jnp.float32
    )
    gain_term = jnp.sum(grad_normed * whitened, axis=(0, 1, 2))
    bias_term = jnp.sum(grad_normed, axis=(0, 1, 2))
    grad_white = grad_normed * gain_f
    grad_conv = inv_std * (
        grad_white
        - jnp.mean(grad_white, axis=-1, keepdims=True)
        - whitened * jnp.mean(grad_white * whitened, axis=-1, keepdims=True)
    )
    kernel_term = kernel_grad(source, grad_conv, extent)
    grad_input = depthwise_back(grad_conv, kernel, extent).astype(jnp.bfloat16)
    return (grad_input, weight_term, kernel_term, gain_term, bias_term)


def body(images, cotangent, depthwise_weight, norm_gain, norm_bias, up_weight):
    weight, kernel_rows, gain_rows, bias_rows = (
        lax.all_gather(up_weight, "shard", axis=0, tiled=True),
        lax.all_gather(depthwise_weight, "shard", axis=0, tiled=True),
        lax.all_gather(norm_gain, "shard", axis=0, tiled=True),
        lax.all_gather(norm_bias, "shard", axis=0, tiled=True),
    )
    grad_input, weight_term, kernel_term, gain_term, bias_term = local_pass(
        images, cotangent, kernel_rows, gain_rows, bias_rows, weight, KS
    )
    depth = weight.shape[0]
    hidden = weight.shape[1]
    taps = KS * KS
    padding = jnp.zeros((depth, 64 - taps - 2), jnp.float32)
    small_term = jnp.concatenate(
        [kernel_term, gain_term[:, None], bias_term[:, None], padding], axis=1
    )
    pixels = (
        images.shape[0]
        * images.shape[1]
        * images.shape[2]
        * lax.axis_size("shard")
        * lax.axis_size("rep")
    )
    factor = 1.0 / math.sqrt(pixels)
    own_rows = depth // lax.axis_size("shard")
    weight_lines = weight_term.reshape(depth * hidden // 128, 128)
    weight_lines, small_share = (
        lax.psum_scatter(weight_lines, "shard", scatter_dimension=0, tiled=True),
        lax.psum_scatter(small_term, "shard", scatter_dimension=0, tiled=True),
    )
    weight_lines, small_share = lax.psum((weight_lines, small_share), "rep")
    weight_share = weight_lines.reshape(own_rows, hidden)
    grad_up = weight_share * factor
    grad_depthwise = small_share[:, :taps] * factor
    grad_gain = small_share[:, taps] * factor
    grad_bias = small_share[:, taps + 1] * factor
    return (grad_input, grad_up, grad_depthwise, grad_gain, grad_bias)


def solution(mesh):
    placed = (
        P(("shard", "rep"), None, None, None),
        P(("shard", "rep"), None, None, None),
        P("shard", None),
        P("shard"),
        P("shard"),
        P("shard", None),
    )
    return jax.shard_map(
        body,
        mesh=mesh,
        in_specs=placed,
        out_specs=(
            P(("shard", "rep"), None, None, None),
            P("shard", None),
            P("shard", None),
            P("shard"),
            P("shard"),
        ),
        check_vma=False,
    )
```

profile of v0, /device:TPU:1, one launch (start us, length us, event | category | flops | bytes accessed | tf_op | source)
XLA Modules:
  0.0 863.3 jit_solution(7494311195742926122)
XLA Ops:
  8.0 1.0 convert_element_type.31
  8.9 140.4 %all-gather = bf16[64,12,49]{2,1,0:T(8,128)(2,1)S(1)} all-gather(bf16[1,12,49]{2,1,0:T(8,128)(2,1)} %bitcast.24), channel_id=1, replica_groups=mesh['shard'=64,'rep'=16] {'shard'}, dimensions={0}, use_global_device_ids=true | all-gather | bytes 76440 | tf_op jit(solution)/shard_map/all_gather | solution.py:111
  149.4 1.4 fusion.108
  153.1 122.4 %all-reduce.6 = (bf16[768]{0:T(1024)(128)(2,1)S(1)}, bf16[768]{0:T(1024)(128)(2,1)S(1)}) all-reduce(bf16[768]{0:T(1024)(128)(2,1)S(1)} %dynamic-update-slice.1, bf16[768]{0:T(1024)(128)(2,1)S(1)} %dynamic-update-slice), channel_id=1, replica_groups=mesh['shard'=64,'rep'=16] {'shard'}, use_global_device_ids=true, to_apply=%add.3 | all-reduce | flops 1536 | bytes 6144
  275.5 2.3 slice_reduce_fusion.46
  277.9 3.8 slice_reduce_fusion.48
  281.9 4.5 slice_reduce_fusion.47
  286.8 4.1 fusion.107
  291.4 3.8 reshape.259
  295.2 1.7 fusion.6
  297.6 3.0 fusion.109
  300.6 5.6 reshape.248
  306.2 2.5 fusion.106
  309.9 1.4 multiply_reduce_fusion.38
  313.4 0.9 stack.204
  314.4 0.9 stack.205
  315.3 0.9 stack.206
  316.2 0.9 stack.207
  317.8 0.9 stack.208
  318.8 0.9 stack.209
  319.7 0.9 stack.210
  322.4 1.0 stack.213
  323.4 0.9 stack.214
  324.3 1.0 stack.215
  326.2 0.9 stack.217
  328.0 0.9 stack.219
  329.0 0.9 stack.220
  331.7 0.9 stack.223
  332.6 0.9 stack.224
  333.6 0.9 stack.225
  334.5 0.9 stack.226
  339.1 0.9 stack.231
  340.0 0.9 stack.232
  341.0 0.9 stack.233
  341.9 0.9 stack.234
  343.7 0.9 stack.236
  344.7 0.9 stack.237
  345.6 0.9 stack.238
  346.5 0.9 stack.239
  348.4 0.9 stack.241
  349.3 0.9 stack.242
  352.9 0.9 broadcast_in_dim.20
  354.7 13.1 %concatenate.3 = f32[768,64]{1,0:T(8,128)} concatenate(f32[768,1]{1,0:T(8,128)S(1)} %stack.196, f32[768,1]{1,0:T(8,128)S(1)} %stack.197, f32[768,1]{1,0:T(8,128)S(1)} %stack.198, f32[768,1]{1,0:T(8,128)S(1)} %stack.199, f32[768,1]{1,0:T(8,128)S(1)} %stack.200, f32[768,1]{1,0:T(8,128)S(1)} %stack.201, f32[768,1]{1,0:T(8,128)S(1)} %stack.202, f32[768,1]{1,0:T(8,128)S(1)} %copy-done, ...), dimensions={1} | concatenate | bytes 393216 | tf_op jit(solution)/shard_map/concatenate | solution.py:122
  367.8 127.5 %fusion = f32[16,64]{1,0:T(8,128)S(1)} fusion(f32[768,64]{1,0:T(8,128)} %concatenate.3), kind=kCustom, calls=%all-reduce-scatter | all-reduce-scatter fusion | flops 65537 | bytes 204800
  495.3 1.3 collective-permute-start.15
  496.6 1.3 collective-permute-start.14
  497.9 1.3 collective-permute-start.13
  499.2 1.4 collective-permute-start.12
  500.6 1.3 collective-permute-start.11
  501.9 1.3 collective-permute-start.10
  503.2 18.2 %collective-permute-start.9 = (f32[16,64]{1,0:T(8,128)S(1)}, f32[16,64]{1,0:T(8,128)S(1)}, u32[]{:S(2)}, u32[]{:S(2)}) collective-permute-start(f32[16,64]{1,0:T(8,128)S(1)} %fusion), channel_id=1, source_target_pairs={{0,160},{16,176},{32,192},{48,208},{64,224},{80,240},{96,256},{112... | collective-permute-start | bytes 12296
  521.4 1.9 collective-permute-start.8
  523.3 9.9 %collective-permute-start.7 = (f32[16,64]{1,0:T(8,128)S(1)}, f32[16,64]{1,0:T(8,128)S(1)}, u32[]{:S(2)}, u32[]{:S(2)}) collective-permute-start(f32[16,64]{1,0:T(8,128)S(1)} %fusion), channel_id=1, source_target_pairs={{0,128},{16,144},{32,160},{48,176},{64,192},{80,208},{96,224},{112... | collective-permute-start | bytes 12296
  533.3 1.7 collective-permute-start.6
  535.0 7.5 collective-permute-start.5
  543.1 1.3 collective-permute-start.4
  544.4 5.0 collective-permute-start.3
  549.4 4.2 collective-permute-start.2
  553.7 1.3 collective-permute-start.1
  555.0 2.8 collective-permute-start
  557.8 4.5 fusion.98
  562.4 1.8 concatenate.4
  564.2 121.5 %psum.15 = f32[12,64]{1,0:T(8,128)S(1)} all-reduce(f32[12,64]{1,0:T(8,128)S(1)} %constant_dynamic-slice_fusion), channel_id=1, replica_groups=mesh['shard'=64,'rep'=16] {'rep'}, use_global_device_ids=true, to_apply=%region_58.59 | all-reduce | flops 768 | bytes 6144 | tf_op jit(solution)/shard_map/psum | solution.py:139
  687.1 168.1 %all-reduce.9.cloned.1.call-done = f32[144,128]{1,0:T(8,128)} async-done(((f32[144,128]{1,0:T(8,128)}), f32[144,128]{1,0:T(8,128)}) %all-reduce.9.cloned.1.call-update) | async-done | bytes 73744 | tf_op jit(solution)/shard_map/psum | solution.py:139
  (161 shorter events, 25.1 us)
Async XLA Ops:
  7.2 284.2 %all-gather.4.cloned.1.call-start = ((), (), s32[]{:S(2)}) async-start(), calls=%async_computation.3 | async-start | bytes 3194880 | tf_op jit(solution)/shard_map/all_gather | solution.py:110
  7.9 678.5 %reduce-scatter.4.cloned.1.call-start = ((), (), s32[]{:S(2)}) async-start(), calls=%async_computation.1 | async-start | bytes 4792320 | tf_op jit(solution)/shard_map/reduce_scatter | solution.py:136
  277.8 8.7 %copy-start.2 = (f32[768]{0:T(1024)}, f32[768]{0:T(1024)S(1)}, u32[]{:S(2)}) copy-start(f32[768]{0:T(1024)S(1)} %get-tuple-element.97) | copy-start | bytes 9220
  277.8 8.7 %copy-start.4 = (f32[768]{0:T(1024)}, f32[768]{0:T(1024)S(1)}, u32[]{:S(2)}) copy-start(f32[768]{0:T(1024)S(1)} %get-tuple-element.98) | copy-start | bytes 9220
  277.8 8.7 %copy-start.6 = (f32[768]{0:T(1024)}, f32[768]{0:T(1024)S(1)}, u32[]{:S(2)}) copy-start(f32[768]{0:T(1024)S(1)} %get-tuple-element.99) | copy-start | bytes 9220
  277.8 8.7 %copy-start.8 = (f32[768]{0:T(1024)}, f32[768]{0:T(1024)S(1)}, u32[]{:S(2)}) copy-start(f32[768]{0:T(1024)S(1)} %get-tuple-element.100) | copy-start | bytes 9220
  277.9 8.7 %copy-start.9 = (f32[768]{0:T(1024)}, f32[768]{0:T(1024)S(1)}, u32[]{:S(2)}) copy-start(f32[768]{0:T(1024)S(1)} %get-tuple-element.101) | copy-start | bytes 9220
  277.9 8.7 %copy-start.10 = (f32[768]{0:T(1024)}, f32[768]{0:T(1024)S(1)}, u32[]{:S(2)}) copy-start(f32[768]{0:T(1024)S(1)} %get-tuple-element.102) | copy-start | bytes 9220
  277.9 8.7 %copy-start.11 = (f32[768]{0:T(1024)}, f32[768]{0:T(1024)S(1)}, u32[]{:S(2)}) copy-start(f32[768]{0:T(1024)S(1)} %get-tuple-element.103) | copy-start | bytes 9220
  277.9 8.7 %copy-start.12 = (f32[768]{0:T(1024)}, f32[768]{0:T(1024)S(1)}, u32[]{:S(2)}) copy-start(f32[768]{0:T(1024)S(1)} %get-tuple-element.104) | copy-start | bytes 9220
  277.9 8.7 %copy-start.13 = (f32[768]{0:T(1024)}, f32[768]{0:T(1024)S(1)}, u32[]{:S(2)}) copy-start(f32[768]{0:T(1024)S(1)} %get-tuple-element.105) | copy-start | bytes 9220
  277.9 8.7 %copy-start.14 = (f32[768]{0:T(1024)}, f32[768]{0:T(1024)S(1)}, u32[]{:S(2)}) copy-start(f32[768]{0:T(1024)S(1)} %get-tuple-element.106) | copy-start | bytes 9220
  281.8 4.9 copy-start.15
  281.8 4.9 copy-start.16
  281.8 4.9 copy-start.17
  281.8 4.9 copy-start.18
  281.8 4.9 copy-start.19
  281.8 4.9 copy-start.20
  281.8 4.9 copy-start.21
  281.8 4.9 copy-start.22
  281.8 4.9 copy-start.23
  281.8 4.9 copy-start.24
  281.9 4.9 copy-start.25
  281.9 4.9 copy-start.26
  281.9 4.9 copy-start.27
  281.9 4.9 copy-start.28
  281.9 4.9 copy-start.29
  281.9 4.9 copy-start.30
  281.9 4.9 copy-start.31
  281.9 4.9 copy-start.32
  281.9 4.9 copy-start.33
  286.5 4.8 copy-start.34
  286.5 4.8 copy-start.35
  286.5 4.8 copy-start.36
  286.5 4.8 copy-start.37
  286.5 4.8 copy-start.38
  286.5 4.8 copy-start.39
  286.5 4.8 copy-start.40
  286.5 4.8 copy-start.41
  286.5 4.8 copy-start.42
  286.5 4.8 copy-start.43
  296.9 0.7 copy-start.1
  306.2 549.0 %all-reduce.9.cloned.1.call-start = ((), (), s32[]{:S(2)}) async-start(), calls=%async_computation.2 | async-start | bytes 147456 | tf_op jit(solution)/shard_map/psum | solution.py:139
  341.9 11.0 %copy-start.44 = (f32[768]{0:T(1024)S(1)}, f32[768]{0:T(1024)}, u32[]{:S(2)}) copy-start(f32[768]{0:T(1024)} %get-tuple-element.55) | copy-start | bytes 9220
  343.7 10.9 %copy-start = (f32[768,1]{1,0:T(8,128)S(1)}, f32[768,1]{1,0:T(8,128)}, u32[]{:S(2)}) copy-start(f32[768,1]{1,0:T(8,128)} %stack.203) | copy-start | bytes 9220
  354.7 203.2 %copy-start.3 = (f32[768]{0:T(1024)S(1)}, f32[768]{0:T(1024)}, u32[]{:S(2)}) copy-start(f32[768]{0:T(1024)} %copy-done.2) | copy-start | bytes 9220
  354.7 203.2 %copy-start.5 = (f32[768]{0:T(1024)S(1)}, f32[768]{0:T(1024)}, u32[]{:S(2)}) copy-start(f32[768]{0:T(1024)} %copy-done.4) | copy-start | bytes 9220
  354.7 203.2 %copy-start.7 = (f32[768]{0:T(1024)S(1)}, f32[768]{0:T(1024)}, u32[]{:S(2)}) copy-start(f32[768]{0:T(1024)} %copy-done.6) | copy-start | bytes 9220
  495.3 6.5 collective-permute-start.15
  496.6 6.6 collective-permute-start.14
  497.9 23.5 %collective-permute-start.13 = (f32[16,64]{1,0:T(8,128)S(1)}, f32[16,64]{1,0:T(8,128)S(1)}, u32[]{:S(2)}, u32[]{:S(2)}) collective-permute-start(f32[16,64]{1,0:T(8,128)S(1)} %fusion), channel_id=1, source_target_pairs={{0,224},{16,240},{32,256},{48,272},{64,288},{80,304},{96,320},{112... | collective-permute-start | bytes 12296
  499.2 24.1 %collective-permute-start.12 = (f32[16,64]{1,0:T(8,128)S(1)}, f32[16,64]{1,0:T(8,128)S(1)}, u32[]{:S(2)}, u32[]{:S(2)}) collective-permute-start(f32[16,64]{1,0:T(8,128)S(1)} %fusion), channel_id=1, source_target_pairs={{0,208},{16,224},{32,240},{48,256},{64,272},{80,288},{96,304},{112... | collective-permute-start | bytes 12296
  500.6 32.7 %collective-permute-start.11 = (f32[16,64]{1,0:T(8,128)S(1)}, f32[16,64]{1,0:T(8,128)S(1)}, u32[]{:S(2)}, u32[]{:S(2)}) collective-permute-start(f32[16,64]{1,0:T(8,128)S(1)} %fusion), channel_id=1, source_target_pairs={{0,192},{16,208},{32,224},{48,240},{64,256},{80,272},{96,288},{112... | collective-permute-start | bytes 12296
  501.9 33.1 %collective-permute-start.10 = (f32[16,64]{1,0:T(8,128)S(1)}, f32[16,64]{1,0:T(8,128)S(1)}, u32[]{:S(2)}, u32[]{:S(2)}) collective-permute-start(f32[16,64]{1,0:T(8,128)S(1)} %fusion), channel_id=1, source_target_pairs={{0,176},{16,192},{32,208},{48,224},{64,240},{80,256},{96,272},{112... | collective-permute-start | bytes 12296
  503.2 39.9 %collective-permute-start.9 = (f32[16,64]{1,0:T(8,128)S(1)}, f32[16,64]{1,0:T(8,128)S(1)}, u32[]{:S(2)}, u32[]{:S(2)}) collective-permute-start(f32[16,64]{1,0:T(8,128)S(1)} %fusion), channel_id=1, source_target_pairs={{0,160},{16,176},{32,192},{48,208},{64,224},{80,240},{96,256},{112... | collective-permute-start | bytes 12296
  521.4 23.1 %collective-permute-start.8 = (f32[16,64]{1,0:T(8,128)S(1)}, f32[16,64]{1,0:T(8,128)S(1)}, u32[]{:S(2)}, u32[]{:S(2)}) collective-permute-start(f32[16,64]{1,0:T(8,128)S(1)} %fusion), channel_id=1, source_target_pairs={{0,144},{16,160},{32,176},{48,192},{64,208},{80,224},{96,240},{112... | collective-permute-start | bytes 12296
  523.3 26.1 %collective-permute-start.7 = (f32[16,64]{1,0:T(8,128)S(1)}, f32[16,64]{1,0:T(8,128)S(1)}, u32[]{:S(2)}, u32[]{:S(2)}) collective-permute-start(f32[16,64]{1,0:T(8,128)S(1)} %fusion), channel_id=1, source_target_pairs={{0,128},{16,144},{32,160},{48,176},{64,192},{80,208},{96,224},{112... | collective-permute-start | bytes 12296
  533.3 20.4 %collective-permute-start.6 = (f32[16,64]{1,0:T(8,128)S(1)}, f32[16,64]{1,0:T(8,128)S(1)}, u32[]{:S(2)}, u32[]{:S(2)}) collective-permute-start(f32[16,64]{1,0:T(8,128)S(1)} %fusion), channel_id=1, source_target_pairs={{0,112},{16,128},{32,144},{48,160},{64,176},{80,192},{96,208},{112... | collective-permute-start | bytes 12296
  535.0 20.0 %collective-permute-start.5 = (f32[16,64]{1,0:T(8,128)S(1)}, f32[16,64]{1,0:T(8,128)S(1)}, u32[]{:S(2)}, u32[]{:S(2)}) collective-permute-start(f32[16,64]{1,0:T(8,128)S(1)} %fusion), channel_id=1, source_target_pairs={{0,96},{16,112},{32,128},{48,144},{64,160},{80,176},{96,192},{112,... | collective-permute-start | bytes 12296
  543.1 19.2 %collective-permute-start.4 = (f32[16,64]{1,0:T(8,128)S(1)}, f32[16,64]{1,0:T(8,128)S(1)}, u32[]{:S(2)}, u32[]{:S(2)}) collective-permute-start(f32[16,64]{1,0:T(8,128)S(1)} %fusion), channel_id=1, source_target_pairs={{0,80},{16,96},{32,112},{48,128},{64,144},{80,160},{96,176},{112,1... | collective-permute-start | bytes 12296
  544.4 17.9 %collective-permute-start.3 = (f32[16,64]{1,0:T(8,128)S(1)}, f32[16,64]{1,0:T(8,128)S(1)}, u32[]{:S(2)}, u32[]{:S(2)}) collective-permute-start(f32[16,64]{1,0:T(8,128)S(1)} %fusion), channel_id=1, source_target_pairs={{0,64},{16,80},{32,96},{48,112},{64,128},{80,144},{96,160},{112,17... | collective-permute-start | bytes 12296
  549.4 12.9 %collective-permute-start.2 = (f32[16,64]{1,0:T(8,128)S(1)}, f32[16,64]{1,0:T(8,128)S(1)}, u32[]{:S(2)}, u32[]{:S(2)}) collective-permute-start(f32[16,64]{1,0:T(8,128)S(1)} %fusion), channel_id=1, source_target_pairs={{0,48},{16,64},{32,80},{48,96},{64,112},{80,128},{96,144},{112,160... | collective-permute-start | bytes 12296
  553.7 8.7 %collective-permute-start.1 = (f32[16,64]{1,0:T(8,128)S(1)}, f32[16,64]{1,0:T(8,128)S(1)}, u32[]{:S(2)}, u32[]{:S(2)}) collective-permute-start(f32[16,64]{1,0:T(8,128)S(1)} %fusion), channel_id=1, source_target_pairs={{0,32},{16,48},{32,64},{48,80},{64,96},{80,112},{96,128},{112,144}... | collective-permute-start | bytes 12296
  555.0 7.4 collective-permute-start
Sparse Core Ops, SparseCore 0:
  10.7 268.6 all-gather.3
  306.3 316.0 reduce-scatter.3
  686.5 168.6 all-reduce.8
where the time goes:
time: 866 us; the launch traced here: 863 us
  blocking collectives  512 us (59%)
  waiting for transfers between devices  169 us (20%)
  local copies, waits for them, and re-layouts  82.3 us (10%)
  starting transfers between devices  61.7 us (7%)
  between operations  16.2 us (2%)
  other arithmetic  15.2 us (2%)
    unnamed x2, blocking collectives  250 us
    psum x1, waiting for transfers between devices, body(): weight_lines, small_share = lax.psum((weight_lines, small_share), 'rep')  168 us
    all_gather x1, blocking collectives, body(): lax.all_gather(depthwise_weight, 'shard', axis=0, tiled=True)  140 us
    psum x1, blocking collectives, body(): weight_lines, small_share = lax.psum((weight_lines, small_share), 'rep')  122 us
    unnamed x16, starting transfers between devices  61.6 us
    another operation x49, local copies, waits for them, and re-layouts, kernel_grad(): return jnp.stack(columns, axis=1)  39.9 us
  transfers between devices with their start and end apart: 19, of which 1 were waited for; matrix products, arithmetic and copies ran while one was open for 25% of the time, Pallas kernels for 0%

commit v1 on v0

v1 whole, which is shorter than its diff:
```python
import functools
import math

import jax
import jax.numpy as jnp
from jax import lax
from jax.experimental import pallas as pl
from jax.experimental.pallas import tpu as pltpu
from jax.sharding import PartitionSpec as P

KS = 7
EPS = 1e-06
F32 = jnp.float32
BF16 = jnp.bfloat16
MESH = pl.DeviceIdType.MESH

NX, NYL, NYH, NZ, NC = 4, 4, 2, 16, 2
NY = NYL * NYH
QUAD = 4
CH = 6


def gelu_slope(v):
    cumulative = 0.5 * (1.0 + lax.erf(v * 0.7071067811865476))
    return cumulative + v * jnp.exp(-0.5 * v * v) * 0.3989422804014327


def kernel(
    factor,
    img_ref, cot_ref, wl_ref,
    gi_ref, gu_ref, sm_ref,
    zbuf, W, S, kT, xp, gp, cv, istd, N, NT, ctr, pre, G, GN, GNr,
    Pf, Pb, F, RB, RF, TB, SX, SXb, RY, SY, K, Kt, Kf, Kb, RK, KS_, ZSf, ZS, RZ, FIN, PC,
    s_z, r_z, s_g2, r_g2, s_wa, r_wa, s_wb, r_wb, s_c, r_c,
    s_m1, r_m1, s_m2, r_m2, s_m3, r_m3, s_y, r_y, s_k, r_k, s_z2, r_z2, s_r1, r_r1, s_r2, r_r2,
):
    s = lax.axis_index("shard")
    r = lax.axis_index("rep")
    yl, z = lax.div(s, NZ), lax.rem(s, NZ)
    x = lax.div(r, NYH * NC)
    yh = lax.rem(lax.div(r, NC), NYH)
    core = lax.rem(r, NC)
    y = yh * NYL + yl
    sgn = 1 - 2 * core
    zq, zr = lax.div(z, QUAD), lax.rem(z, QUAD)
    source = zq == x

    def dev(x_, y_, z_, c_):
        return (
            lax.rem(y_, NYL) * NZ + z_,
            x_ * (NYH * NC) + lax.div(y_, NYL) * NC + c_,
        )

    def dz(k):
        return dev(x, y, lax.rem(z + k, NZ), core)

    def dxy(dx, dy):
        return dev(lax.rem(x + dx + 2 * NX, NX), lax.rem(y + dy + 2 * NY, NY), z, core)

    sib = dev(x, y, z, 1 - core)

    def rcopy(src, dst, ss, rs, to):
        return pltpu.make_async_remote_copy(
            src_ref=src, dst_ref=dst, send_sem=ss, recv_sem=rs, device_id=to, device_id_type=MESH
        )

    barrier = pltpu.get_barrier_semaphore()

    def hello(to):
        pl.semaphore_signal(barrier, inc=1, device_id=to, device_id_type=MESH)

    @pl.loop(1, NZ)
    def _(k):
        hello(dz(k))

    @pl.loop(1, NX * NY)
    def _(k):
        hello(dxy(lax.div(k, NY), lax.rem(k, NY)))

    hello(sib)
    hello(dev(x, lax.rem(y + NYL, NY), z, 1 - core))
    pl.semaphore_wait(barrier, (NZ - 1) + (NX * NY - 1) + 2)

    def z_send(k):
        return rcopy(wl_ref.at[core], zbuf.at[zr], s_z.at[k - 1], r_z.at[zr], dz(k))

    @pl.when(source)
    def _():
        @pl.loop(1, NZ)
        def _(k):
            z_send(k).start()

    half_own = pl.ds(pl.multiple_of(core * 768, 128), 768)
    half_sib = pl.ds(pl.multiple_of((1 - core) * 768, 128), 768)
    cot_send = rcopy(cot_ref.at[:, half_sib], ctr, s_c.at[0], r_c.at[0], sib)
    cot_send.start()

    @pl.when(source)
    def _():
        zbuf[zr] = wl_ref[core]

    zero_edge = jnp.zeros((8, 8, 128), F32)
    for ck in range(CH):
        xp[ck, :, 0:8, :] = zero_edge
        xp[ck, :, 24:32, :] = zero_edge
        gp[ck, :, 0:8, :] = zero_edge
        gp[ck, :, 24:32, :] = zero_edge
        xp[ck, :, 8:24, :] = img_ref[:, :, ck * 128 : (ck + 1) * 128].astype(F32)
    K[...] = jnp.zeros_like(K)
    ZSf[...] = jnp.zeros_like(ZSf)

    for j in range(QUAD):
        @pl.when(jnp.logical_not(jnp.logical_and(source, zr == j)))
        def _():
            rcopy(wl_ref.at[core], zbuf.at[j], s_z.at[0], r_z.at[j], sib).wait_recv()

    rows = lax.broadcasted_iota(jnp.int32, (48, 64), 0)
    cols = lax.broadcasted_iota(jnp.int32, (48, 64), 1)
    pick48 = jnp.where(rows // 12 * 16 + rows % 12 == cols, 1.0, 0.0).astype(BF16)
    packed = jnp.dot(pick48, zbuf[...].reshape(64, 896), preferred_element_type=F32).astype(BF16)
    W[yl, x] = packed[:, :768]
    S[yl, x] = packed[:, 768:]

    def dy_of(i):
        return (0, 1, -1, 2 * sgn)[i]

    def small_send(k):
        return rcopy(
            S.at[yl, x], S.at[yl, x], s_g2.at[k - 1], r_g2.at[k - 1], dxy(k // 4, dy_of(k % 4))
        )

    smalls = [small_send(k) for k in range(1, 16)]
    for c in smalls:
        c.start()
    A, B = pl.ds(0, 384), pl.ds(384, 384)
    a2 = [
        rcopy(W.at[yl, x, :, A], W.at[yl, x, :, A], s_wa.at[i], r_wa.at[i], dxy(0, dy_of(i + 1)))
        for i in range(3)
    ]
    b2 = [
        rcopy(W.at[yl, x, :, B], W.at[yl, x, :, B], s_wb.at[i], r_wb.at[i], dxy(i + 1, 0))
        for i in range(3)
    ]
    for i in range(3):
        a2[i].start()
        b2[i].start()

    for c in smalls:
        c.wait_recv()
    for c in a2:
        c.wait_recv()
    xf = lax.rem(x + sgn + NX, NX)
    xb = lax.rem(x - sgn + NX, NX)
    to_f, to_b = dxy(sgn, 0), dxy(-sgn, 0)
    a3 = [
        rcopy(W.at[:, x, :, A], W.at[:, x, :, A], s_wa.at[3], r_wa.at[3], to_f),
        rcopy(W.at[:, x, :, A], W.at[:, x, :, A], s_wa.at[4], r_wa.at[4], to_b),
    ]
    a3[0].start()
    a3[1].start()
    for c in b2:
        c.wait_recv()
    b3 = [
        rcopy(W.at[yl, :, :, B], W.at[yl, :, :, B], s_wb.at[3 + i], r_wb.at[3 + i], dxy(0, dy_of(i + 1)))
        for i in range(3)
    ]
    for c in b3:
        c.start()
    a3_fwd = rcopy(W.at[:, xb, :, A], W.at[:, xb, :, A], s_wa.at[5], r_wa.at[5], to_f)

    kcols = jnp.transpose(S[...].reshape(768, 128).astype(F32))
    for ck in range(CH):
        kT[ck] = kcols[:64, ck * 128 : (ck + 1) * 128]

    a3[0].wait_recv()
    a3_fwd.start()

    @pl.loop(0, CH)
    def _(ck):
        acc = [jnp.zeros((16, 128), F32) for _ in range(8)]
        for b in range(KS):
            taps = [kT[ck, pl.ds(a * KS + b, 1), :] for a in range(KS)]
            for row in range(8):
                xs = xp[ck, row, pl.ds(5 + b, 16), :]
                for a in range(KS):
                    h = row - a + 3
                    if 0 <= h < 8:
                        acc[h] = acc[h] + xs * taps[a]
        for h in range(8):
            cv[ck, h] = acc[h]

    @pl.loop(0, 8)
    def _(h):
        v = [cv[ck, h] for ck in range(CH)]
        total = v[0]
        for ck in range(1, CH):
            total = total + v[ck]
        avg = jnp.sum(total, axis=-1, keepdims=True) * (1.0 / 768)
        v = [u - avg for u in v]
        total = v[0] * v[0]
        for ck in range(1, CH):
            total = total + v[ck] * v[ck]
        inv = lax.rsqrt(jnp.sum(total, axis=-1, keepdims=True) * (1.0 / 768) + EPS)
        istd[h] = jnp.broadcast_to(inv, (16, 128))
        for ck in range(CH):
            w = v[ck] * inv
            cv[ck, h] = w
            N[core, pl.ds(pl.multiple_of(h * 16, 16), 16), ck * 128 : (ck + 1) * 128] = (
                w * kT[ck, 49:50, :] + kT[ck, 50:51, :]
            ).astype(BF16)

    n_send = rcopy(N.at[core], N.at[core], s_c.at[1], r_c.at[1], sib)
    n_send.start()
    cot_send.wait_recv()
    n_send.wait_recv()
    NT[...] = jnp.transpose(N[...].reshape(256, 768).astype(F32)).astype(BF16)

    def pointwise(cols, waits):
        for c in waits:
            c.wait_recv()
        pre[:, cols] = jnp.dot(
            N[...].reshape(256, 768), W[:, :, :, cols].reshape(768, 384), preferred_element_type=F32
        )

    pointwise(slice(384, 768), b3)
    pointwise(slice(0, 384), [a3[1], a3_fwd])

    @pl.loop(0, 8)
    def _(i):
        at = pl.ds(pl.multiple_of(i * 16, 16), 16)
        slope = gelu_slope(pre[pl.ds(pl.multiple_of(core * 128 + i * 16, 16), 16), :])
        G[core, at, :] = (cot_ref[at, half_own].astype(F32) * slope).astype(BF16)
        slope = gelu_slope(pre[pl.ds(pl.multiple_of((1 - core) * 128 + i * 16, 16), 16), :])
        G[1 - core, at, :] = (ctr[at, :].astype(F32) * slope).astype(BF16)

    def m1(j, q):
        return rcopy(Pb.at[q, lax.rem(x + 2, NX)], F.at[j], s_m1.at[j], r_m1.at[j], to_f)

    def m2(j, q):
        return rcopy(Pb.at[q, xb], RB.at[j], s_m2.at[j], r_m2.at[j], to_b)

    def m3(j):
        return rcopy(TB.at[j], RF.at[j], s_m3.at[j], r_m3.at[j], to_f)

    order = (2, 3, 1, 0)
    pieces = [(j, lax.rem(yl + j, NYL)) for j in order]
    for j, q in pieces:
        part = jnp.dot(
            NT[pl.ds(pl.multiple_of(q * 192, 64), 192), :], G[...].reshape(256, 768),
            preferred_element_type=F32,
        ).reshape(QUAD, 48, 768)
        Pf[q] = part
        Pb[q] = part.astype(BF16)
        m1(j, q).start()
        m2(j, q).start()

    GN[...] = lax.dot_general(
        G[...].reshape(256, 768), W[...].reshape(768, 768), (((1,), (1,)), ((), ())),
        preferred_element_type=F32,
    ).reshape(2, 128, 768)
    gn_send = rcopy(GN.at[1 - core], GNr, s_c.at[2], r_c.at[2], sib)
    gn_send.start()

    def forward_m3(j, q):
        m1(j, q).wait_recv()
        TB[j] = (F[j].astype(F32) + Pf[q, xf]).astype(BF16)
        m3(j).start()

    for j, q in pieces:
        forward_m3(j, q)

    gn_send.wait_recv()

    def ln_back(h, carry):
        at = pl.ds(pl.multiple_of(h * 16, 16), 16)
        sums_g, sums_b = carry
        gn = [
            GN[core, at, ck * 128 : (ck + 1) * 128] + GNr[at, ck * 128 : (ck + 1) * 128]
            for ck in range(CH)
        ]
        wh = [cv[ck, h] for ck in range(CH)]
        sums_b = [a + g for a, g in zip(sums_b, gn)]
        sums_g = [a + g * w for a, g, w in zip(sums_g, gn, wh)]
        gw = [g * kT[ck, 49:50, :] for ck, g in enumerate(gn)]
        t1, t2 = gw[0], gw[0] * wh[0]
        for ck in range(1, CH):
            t1 = t1 + gw[ck]
            t2 = t2 + gw[ck] * wh[ck]
        m_1 = jnp.sum(t1, axis=-1, keepdims=True) * (1.0 / 768)
        m_2 = jnp.sum(t2, axis=-1, keepdims=True) * (1.0 / 768)
        inv = istd[h]
        for ck in range(CH):
            gp[ck, h, 8:24, :] = inv * (gw[ck] - m_1 - wh[ck] * m_2)
        return sums_g, sums_b

    zeros = [jnp.zeros((16, 128), F32) for _ in range(CH)]
    sums_g, sums_b = lax.fori_loop(0, 8, ln_back, (zeros, zeros))
    for ck in range(CH):
        K[ck, 49:50, :] = jnp.sum(sums_g[ck], axis=0, keepdims=True)
        K[ck, 50:51, :] = jnp.sum(sums_b[ck], axis=0, keepdims=True)

    @pl.loop(0, CH)
    def _(ck):
        g = [gp[ck, h, 8:24, :] for h in range(8)]
        for b in range(KS):
            acc = [None] * KS
            for row in range(8):
                xs = xp[ck, row, pl.ds(5 + b, 16), :]
                for a in range(KS):
                    h = row - a + 3
                    if 0 <= h < 8:
                        t = xs * g[h]
                        acc[a] = t if acc[a] is None else acc[a] + t
            for a in range(KS):
                K[ck, a * KS + b : a * KS + b + 1, :] = jnp.sum(acc[a], axis=0, keepdims=True)

    for ck in range(CH):
        Kt[ck * 128 : (ck + 1) * 128, :] = jnp.transpose(K[ck])
    kt = Kt[...].reshape(NYL, QUAD, 48, 128)
    Kf[...] = kt
    Kb[...] = kt.astype(BF16)

    def small_out(k):
        qx, ql = lax.rem(x + k // 4, NX), lax.rem(yl + k % 4, NYL)
        return rcopy(
            Kb.at[ql, qx], RK.at[k - 1], s_k.at[k - 1], r_k.at[k - 1], dev(qx, yh * NYL + ql, z, core)
        )

    outs = [small_out(k) for k in range(1, 16)]
    for c in outs:
        c.start()

    def y_send(j, q, d):
        y_to = lax.rem(y + d, NY)
        cols = pl.ds(pl.multiple_of(lax.div(y_to, NYL) * 384, 128), 384)
        return rcopy(SXb.at[q, :, cols], RY.at[d], s_y.at[d], r_y.at[d], dxy(0, d))

    for j, q in pieces:
        m2(j, q).wait_recv()
        m3(j).wait_recv()
        total = Pf[q, x] + RB[j].astype(F32) + RF[j].astype(F32)
        SXb[q] = total.astype(BF16)
        for d in (j, j + 4):
            if d:
                y_send(j, q, d).start()
        if j == 0:
            SX[...] = total

    @pl.loop(0, CH)
    def _(ck):
        acc = [jnp.zeros((16, 128), F32) for _ in range(8)]
        for b in range(KS):
            taps = [kT[ck, pl.ds(a * KS + b, 1), :] for a in range(KS)]
            for row in range(8):
                gs = gp[ck, row, pl.ds(11 - b, 16), :]
                for a in range(KS):
                    h = row + a - 3
                    if 0 <= h < 8:
                        acc[h] = acc[h] + gs * taps[a]
        lanes = pl.ds(pl.multiple_of(ck * 128, 128), 128)
        for h in range(8):
            gi_ref[h, :, lanes] = acc[h].astype(BF16)

    for c in outs:
        c.wait_recv()
    ksum = Kf[yl, x]
    for k in range(15):
        ksum = ksum + RK[k].astype(F32)
    KS_[...] = ksum
    own_cols = pl.ds(pl.multiple_of(yh * 384, 128), 384)
    for j, q in pieces:
        for d in (j, j + 4):
            if d:
                y_send(j, q, d).wait_recv()
    ysum = SX[:, own_cols]
    for d in range(1, NY):
        ysum = ysum + RY[d].astype(F32)
    SY[...] = ysum
    for j in range(QUAD):
        ZSf[j, 0:12, 0:384] = SY[12 * j : 12 * j + 12, :]
        ZSf[j, 0:12, 384:512] = KS_[12 * j : 12 * j + 12, :]
    ZS[...] = ZSf[...].astype(BF16)

    def z2_send(j):
        return rcopy(
            ZS.at[j], RZ.at[z], s_z2.at[j], r_z2.at[z], dev(x, y, x * QUAD + j, core)
        )

    for j in range(QUAD):
        @pl.when(x * QUAD + j != z)
        def _():
            z2_send(j).start()

    p = yh * NC + core

    def r1_send(i):
        return rcopy(FIN, PC.at[p], s_r1.at[i - 1], r_r1, dxy(i, 0))

    @pl.when(source)
    def _():
        RZ[z] = ZS[zr]

        @pl.loop(1, NZ)
        def _(k):
            frm = lax.rem(z + k, NZ)
            rcopy(ZS.at[0], RZ.at[frm], s_z2.at[0], r_z2.at[frm], sib).wait_recv()

        total = RZ[0].astype(F32)
        for k in range(1, NZ):
            total = total + RZ[k].astype(F32)
        FIN[...] = total * factor
        for i in range(1, NX):
            r1_send(i).start()
        PC[p] = total * factor

    @pl.when(jnp.logical_not(source))
    def _():
        r1_send(1).wait_recv()

    def r2_send(k):
        yh_to = (yh, 1 - yh)[k // 2]
        c_to = (core, 1 - core)[k % 2]
        return rcopy(PC.at[p], PC.at[p], s_r2.at[k - 1], r_r2.at[k - 1], dev(x, yh_to * NYL + yl, z, c_to))

    r2 = [r2_send(k) for k in range(1, 4)]
    for c in r2:
        c.start()
    for c in r2:
        c.wait_recv()
    for q in range(4):
        at = (q % NC) * 768 + (q // NC) * 384
        gu_ref[:, at : at + 384] = PC[q, 0:12, 0:384]
    sm_ref[...] = (PC[0, 0:12, 384:] + PC[1, 0:12, 384:]) + (PC[2, 0:12, 384:] + PC[3, 0:12, 384:])

    @pl.when(source)
    def _():
        @pl.loop(1, NZ)
        def _(k):
            z_send(k).wait_send()

        for i in range(1, NX):
            r1_send(i).wait_send()

    for c in [cot_send, n_send, gn_send, a3_fwd] + smalls + a2 + b2 + a3 + b3 + outs + r2:
        c.wait_send()
    for j, q in pieces:
        m1(j, q).wait_send()
        m2(j, q).wait_send()
        m3(j).wait_send()
        for d in (j, j + 4):
            if d:
                y_send(j, q, d).wait_send()
    for j in range(QUAD):
        @pl.when(x * QUAD + j != z)
        def _():
            z2_send(j).wait_send()


def body(images, cotangent, depthwise_weight, norm_gain, norm_bias, up_weight):
    pixels = (
        images.shape[0] * images.shape[1] * images.shape[2]
        * lax.axis_size("shard") * lax.axis_size("rep")
    )
    factor = 1.0 / math.sqrt(pixels)
    small = jnp.concatenate(
        [depthwise_weight, norm_gain[:, None], norm_bias[:, None], jnp.zeros((12, 77), BF16)], axis=1
    )
    block = jnp.stack(
        [jnp.concatenate([up_weight[:, :768], small], 1), jnp.concatenate([up_weight[:, 768:], small], 1)]
    )
    block = jnp.pad(block, ((0, 0), (0, 4), (0, 0)))
    dma = pltpu.SemaphoreType.DMA
    vm = lambda dtype, *shape: pltpu.VMEM(shape, dtype)
    gi, gu, sm = pl.pallas_call(
        functools.partial(kernel, factor),
        out_shape=(
            jax.ShapeDtypeStruct((8, 16, 768), BF16),
            jax.ShapeDtypeStruct((12, 1536), F32),
            jax.ShapeDtypeStruct((12, 128), F32),
        ),
        in_specs=[pl.BlockSpec(memory_space=pltpu.VMEM)] * 3,
        out_specs=[pl.BlockSpec(memory_space=pltpu.VMEM)] * 3,
        scratch_shapes=[
            vm(BF16, 4, 16, 896),
            vm(BF16, 4, 4, 48, 768),
            vm(BF16, 4, 4, 48, 128),
            vm(F32, CH, 64, 128),
            vm(F32, CH, 8, 32, 128),
            vm(F32, CH, 8, 32, 128),
            vm(F32, CH, 8, 16, 128),
            vm(F32, 8, 16, 128),
            vm(BF16, 2, 128, 768),
            vm(BF16, 768, 256),
            vm(BF16, 128, 768),
            vm(F32, 256, 768),
            vm(BF16, 2, 128, 768),
            vm(F32, 2, 128, 768),
            vm(F32, 128, 768),
            vm(F32, 4, 4, 48, 768),
            vm(BF16, 4, 4, 48, 768),
            vm(BF16, 4, 48, 768),
            vm(BF16, 4, 48, 768),
            vm(BF16, 4, 48, 768),
            vm(BF16, 4, 48, 768),
            vm(F32, 48, 768),
            vm(BF16, 4, 48, 768),
            vm(BF16, 8, 48, 384),
            vm(F32, 48, 384),
            vm(F32, CH, 128, 128),
            vm(F32, 768, 128),
            vm(F32, 4, 4, 48, 128),
            vm(BF16, 4, 4, 48, 128),
            vm(BF16, 15, 48, 128),
            vm(F32, 48, 128),
            vm(F32, 4, 16, 512),
            vm(BF16, 4, 16, 512),
            vm(BF16, 16, 16, 512),
            vm(F32, 16, 512),
            vm(F32, 4, 16, 512),
            dma((15,)), dma((4,)),
            dma((15,)), dma((15,)),
            dma((6,)), dma((6,)),
            dma((6,)), dma((6,)),
            dma((3,)), dma((3,)),
            dma((4,)), dma((4,)),
            dma((4,)), dma((4,)),
            dma((4,)), dma((4,)),
            dma((8,)), dma((8,)),
            dma((15,)), dma((15,)),
            dma((4,)), dma((16,)),
            dma((3,)), dma,
            dma((3,)), dma((3,)),
        ],
        compiler_params=pltpu.CompilerParams(
            collective_id=0, has_side_effects=True, vmem_limit_bytes=40 << 20
        ),
    )(images.reshape(8, 16, 768), cotangent.reshape(128, 1536), block)
    taps = KS * KS
    return (gi.reshape(images.shape), gu, sm[:, :taps], sm[:, taps], sm[:, taps + 1])


def solution(mesh):
    placed = (
        P(("shard", "rep"), None, None, None),
        P(("shard", "rep"), None, None, None),
        P("shard", None),
        P("shard"),
        P("shard"),
        P("shard", None),
    )
    return jax.shard_map(
        body,
        mesh=mesh,
        in_specs=placed,
        out_specs=(
            P(("shard", "rep"), None, None, None),
            P("shard", None),
            P("shard", None),
            P("shard"),
            P("shard"),
        ),
        check_vma=False,
    )
```

time: 866 us -> 108 us (0.12)
  the two profiles are of different devices: /device:TPU:1 before, /device:TPU:5 now
where the time goes in v1:
time: 108 us
  Pallas kernels  99.4 us (92%)
  local copies, waits for them, and re-layouts  7.48 us (7%)
    pallas_call x1, Pallas kernels, body(): pl.pallas_call(functools.partial(kernel, factor), out_shape=(jax.ShapeDty...  99.4 us
    unnamed x7, local copies, waits for them, and re-layouts  2.91 us

profile of v1, /device:TPU:5, one launch (start us, length us, event | category | flops | bytes accessed | tf_op | source)
XLA Modules:
  0.0 107.6 jit_solution(8732079205176494453)
XLA Ops:
  0.6 0.0 copy-start.1
  0.6 0.8 copy.15
  1.4 0.8 copy.16
  2.2 0.8 fusion.3
  3.0 0.8 concatenate.9
  3.7 0.8 concatenate.10
  4.5 0.0 copy-done.1
  4.5 0.0 copy-start
  4.6 1.0 copy-done
  5.5 99.4 %shard_map.101 = (bf16[8,16,768]{2,1,0:T(8,128)(2,1)S(1)}, f32[12,1536]{1,0:T(8,128)S(1)}, f32[12,128]{1,0:T(8,128)S(1)}) custom-call(bf16[8,16,768]{2,1,0:T(8,128)(2,1)S(1)} %bitcast.10, bf16[128,1536]{1,0:T(8,128)(2,1)S(1)} %bitcast.8, bf16[2,16,896]{2,1,0:T(8,128)(2,1)S(1)} %fusion.2.wl_ref), custom_call_target="tpu_custom_call" | custom-call | tf_op jit(solution)/shard_map/pallas_call | solution.py:474
  105.0 0.7 slice_reduce_fusion
  105.7 0.7 copy.22
  106.3 0.6 copy.23
  107.0 0.6 copy.24
  (2 shorter events, 0.0 us)
Async XLA Ops:
  0.6 3.9 %copy-start.1 = (bf16[1,8,16,768]{3,2,1,0:T(8,128)(2,1)S(1)}, bf16[1,8,16,768]{3,2,1,0:T(8,128)(2,1)}, u32[]{:S(2)}) copy-start(bf16[1,8,16,768]{3,2,1,0:T(8,128)(2,1)} %param.6) | copy-start | bytes 589828
  4.5 1.0 copy-start

commit v2 on v1

v2 whole, which is shorter than its diff:
```python
import math

import jax
import jax.numpy as jnp
from jax import lax
from jax.experimental import pallas as pl
from jax.experimental.pallas import tpu as pltpu
from jax.sharding import PartitionSpec as P

KS = 7
EPS = 1e-06
F32 = jnp.float32
BF16 = jnp.bfloat16
MESH = pl.DeviceIdType.MESH

NX, NYL, NYH, NZ, NC = 4, 4, 2, 16, 2
NY = NYL * NYH
QUAD = 4
CH = 6


def gelu_slope(v):
    cumulative = 0.5 * (1.0 + lax.erf(v * 0.7071067811865476))
    return cumulative + v * jnp.exp(-0.5 * v * v) * 0.3989422804014327


def kernel(
    img_hbm, cot_hbm, dw_hbm, gain_hbm, bias_hbm, up_hbm,
    gi_hbm, gu_ref, sm_ref,
    gi_ref, imgv, upv, dwv, gnv, bsv, wlf, wl, zall,
    zbuf, W, S, kT, xp, gp, cv, istd, N, NT, Ct, pre, G, GN, GNr,
    Pf, Pb, F, RB, RF, TB, SX, SXb, RY, SY, K, Kt, Kf, Kb, RK, KS_, ZSf, ZS, RZ, FIN, PC,
    s_in, s_z, r_z, s_g2, r_g2, s_w, r_w, s_c, r_c,
    s_m, r_m1, r_m2, r_m3, s_y, r_y, s_k, r_k, s_z2, r_z2, s_r1, r_r1, s_r2, r_r2,
):
    s = lax.axis_index("shard")
    r = lax.axis_index("rep")
    yl, z = lax.div(s, NZ), lax.rem(s, NZ)
    x = lax.div(r, NYH * NC)
    yh = lax.rem(lax.div(r, NC), NYH)
    core = lax.rem(r, NC)
    y = yh * NYL + yl
    sgn = 1 - 2 * core
    zq, zr = lax.div(z, QUAD), lax.rem(z, QUAD)
    source = zq == x

    def dev(x_, y_, z_, c_):
        return (
            lax.rem(y_, NYL) * NZ + z_,
            x_ * (NYH * NC) + lax.div(y_, NYL) * NC + c_,
        )

    def dz(k):
        return dev(x, y, lax.rem(z + k, NZ), core)

    def dxy(dx, dy):
        return dev(lax.rem(x + dx + 2 * NX, NX), lax.rem(y + dy + 2 * NY, NY), z, core)

    sib = dev(x, y, z, 1 - core)
    far = dev(x, lax.rem(y + NYL, NY), z, 1 - core)

    def rcopy(src, dst, ss, rs, to):
        return pltpu.make_async_remote_copy(
            src_ref=src, dst_ref=dst, send_sem=ss, recv_sem=rs, device_id=to, device_id_type=MESH
        )

    def landed(ref, sem):
        rcopy(ref, ref, s_in.at[0], sem, sib).wait_recv()

    def left(ref, sem):
        rcopy(ref, ref, sem, s_in.at[0], sib).wait_send()

    def dy_of(i):
        return (0, 1, -1, 2 * sgn)[i]

    half_own = pl.ds(pl.multiple_of(core * 768, 128), 768)
    half_sib = pl.ds(pl.multiple_of((1 - core) * 768, 128), 768)

    barrier = pltpu.get_barrier_semaphore()

    def hello(to):
        pl.semaphore_signal(barrier, inc=1, device_id=to, device_id_type=MESH)

    @pl.when(source)
    def _():
        @pl.loop(1, NZ)
        def _(k):
            hello(dz(k))

    @pl.when(jnp.logical_not(source))
    def _():
        for j in range(QUAD):
            hello(dev(x, y, x * QUAD + j, core))

    loads = [
        pltpu.make_async_copy(src, dst, s_in.at[i])
        for i, (src, dst) in enumerate(
            [(up_hbm, upv), (dw_hbm, dwv), (gain_hbm, gnv), (bias_hbm, bsv), (img_hbm, imgv),
             (cot_hbm.at[:, half_own], Ct.at[core])]
        )
    ]
    for c in loads:
        c.start()
    for d in range(1, NY):
        hello(dxy(0, d))
    for dx in range(1, NX):
        for i in range(4):
            hello(dxy(-dx, -dy_of(i)))
    hello(sib)
    hello(far)

    wlf[...] = jnp.zeros_like(wlf)
    for c in loads[:4]:
        c.wait()
    wlf[0:12, 0:768] = upv[:, half_own].astype(F32)
    wlf[0:12, 768:817] = dwv[...].astype(F32)
    row12 = lax.broadcasted_iota(jnp.int32, (12, 12), 0)
    col12 = lax.broadcasted_iota(jnp.int32, (12, 12), 1)

    def column(v):
        return jnp.sum(jnp.where(row12 == col12, v[...].astype(F32), 0.0), axis=1, keepdims=True)

    lane = lax.broadcasted_iota(jnp.int32, (12, 128), 1)
    extra = jnp.where(lane == 49, column(gnv), jnp.where(lane == 50, column(bsv), 0.0))
    wlf[0:12, 768:896] = wlf[0:12, 768:896] + extra
    wl[...] = wlf[...].astype(BF16)
    pl.semaphore_wait(barrier, 25 + 11 * source.astype(jnp.int32))

    @pl.when(source)
    def _():
        @pl.loop(1, NZ)
        def _(k):
            rcopy(wl, zbuf.at[zr], s_z, r_z, dz(k)).start()

        zbuf[zr] = wl[...]

    cot_send = rcopy(cot_hbm.at[:, half_sib], Ct.at[core], s_c.at[0], r_c.at[0], sib)
    cot_send.start()

    zero_edge = jnp.zeros((8, 8, 128), F32)
    loads[4].wait()
    for ck in range(CH):
        xp[ck, :, 0:8, :] = zero_edge
        xp[ck, :, 24:32, :] = zero_edge
        gp[ck, :, 0:8, :] = zero_edge
        gp[ck, :, 24:32, :] = zero_edge
        xp[ck, :, 8:24, :] = imgv[:, :, ck * 128 : (ck + 1) * 128].astype(F32)
    K[...] = jnp.zeros_like(K)
    ZSf[...] = jnp.zeros_like(ZSf)
    loads[5].wait()

    @pl.when(source)
    def _():
        landed(zbuf.at[pl.ds(0, 3)], r_z)

    @pl.when(jnp.logical_not(source))
    def _():
        landed(zbuf, r_z)

    rows = lax.broadcasted_iota(jnp.int32, (48, 64), 0)
    cols = lax.broadcasted_iota(jnp.int32, (48, 64), 1)
    pick48 = jnp.where(rows // 12 * 16 + rows % 12 == cols, 1.0, 0.0).astype(BF16)
    packed = jnp.dot(pick48, zbuf[...].reshape(64, 896), preferred_element_type=F32)
    W[yl, x] = packed[:, :768].astype(BF16)
    slot = yl * QUAD + x
    S[slot] = (packed[0:24, 768:] + pltpu.roll(packed[24:48, 768:], 64, 1)).astype(BF16)

    for k in range(1, 16):
        rcopy(S.at[slot], S.at[slot], s_g2, r_g2, dxy(k // 4, dy_of(k % 4))).start()
    A, B = pl.ds(0, 384), pl.ds(384, 384)
    for i in range(1, 4):
        rcopy(W.at[yl, x, :, A], W.at[yl, x, :, A], s_w.at[0], r_w.at[0], dxy(0, dy_of(i))).start()
        rcopy(W.at[yl, x, :, B], W.at[yl, x, :, B], s_w.at[1], r_w.at[1], dxy(i, 0)).start()

    landed(W.at[0, pl.ds(0, 3), :, A], r_w.at[0])
    for i in range(1, 4):
        rcopy(W.at[:, x, :, A], W.at[:, x, :, A], s_w.at[2], r_w.at[2], dxy(i, 0)).start()
    landed(W.at[0, pl.ds(0, 3), :, B], r_w.at[1])
    for i in range(1, 4):
        rcopy(W.at[yl, :, :, B], W.at[yl, :, :, B], s_w.at[3], r_w.at[3], dxy(0, dy_of(i))).start()

    landed(S.at[pl.ds(0, 15)], r_g2)
    flat = S[...].astype(F32)
    other = pltpu.roll(flat.reshape(384, 128), 64, 1).reshape(16, 24, 128)
    kcols = jnp.transpose(jnp.concatenate([flat, other], axis=1).reshape(768, 128))
    for ck in range(CH):
        kT[ck] = kcols[:64, ck * 128 : (ck + 1) * 128]

    @pl.loop(0, CH)
    def _(ck):
        acc = [jnp.zeros((16, 128), F32) for _ in range(8)]
        for b in range(KS):
            taps = [kT[ck, pl.ds(a * KS + b, 1), :] for a in range(KS)]
            for row in range(8):
                xs = xp[ck, row, pl.ds(5 + b, 16), :]
                for a in range(KS):
                    h = row - a + 3
                    if 0 <= h < 8:
                        acc[h] = acc[h] + xs * taps[a]
        for h in range(8):
            cv[ck, h] = acc[h]

    @pl.loop(0, 8)
    def _(h):
        v = [cv[ck, h] for ck in range(CH)]
        total = v[0]
        for ck in range(1, CH):
            total = total + v[ck]
        avg = jnp.sum(total, axis=-1, keepdims=True) * (1.0 / 768)
        v = [u - avg for u in v]
        total = v[0] * v[0]
        for ck in range(1, CH):
            total = total + v[ck] * v[ck]
        inv = lax.rsqrt(jnp.sum(total, axis=-1, keepdims=True) * (1.0 / 768) + EPS)
        istd[h] = jnp.broadcast_to(inv, (16, 128))
        for ck in range(CH):
            w = v[ck] * inv
            cv[ck, h] = w
            N[core, pl.ds(pl.multiple_of(h * 16, 16), 16), ck * 128 : (ck + 1) * 128] = (
                w * kT[ck, 49:50, :] + kT[ck, 50:51, :]
            ).astype(BF16)

    n_send = rcopy(N.at[core], N.at[core], s_c.at[1], r_c.at[1], sib)
    n_send.start()

    def flip(c):
        NT[:, pl.ds(pl.multiple_of(c * 128, 128), 128)] = jnp.transpose(N[c].astype(F32)).astype(BF16)

    flip(core)
    n_send.wait_recv()
    flip(1 - core)
    cot_send.wait_recv()

    def pointwise(cols):
        pre[:, cols] = jnp.dot(
            N[...].reshape(256, 768), W[:, :, :, cols].reshape(768, 384), preferred_element_type=F32
        )

    landed(W.at[pl.ds(0, 3), :, :, A], r_w.at[2])
    pointwise(slice(0, 384))
    landed(W.at[pl.ds(0, 3), :, :, B], r_w.at[3])
    pointwise(slice(384, 768))

    @pl.loop(0, 8)
    def _(i):
        at = pl.ds(pl.multiple_of(i * 16, 16), 16)
        for c in range(2):
            slope = gelu_slope(pre[pl.ds(pl.multiple_of(c * 128 + i * 16, 16), 16), :])
            G[c, at, :] = (Ct[c, at, :].astype(F32) * slope).astype(BF16)

    xf = lax.rem(x + sgn + NX, NX)
    xb = lax.rem(x - sgn + NX, NX)
    to_f, to_b = dxy(sgn, 0), dxy(-sgn, 0)
    pieces = [(j, lax.rem(yl + j, NYL)) for j in (2, 3, 1, 0)]
    for j, q in pieces:
        part = jnp.dot(
            NT[pl.ds(pl.multiple_of(q * 192, 64), 192), :], G[...].reshape(256, 768),
            preferred_element_type=F32,
        ).reshape(QUAD, 48, 768)
        Pf[q] = part
        Pb[q] = part.astype(BF16)
        rcopy(Pb.at[q, lax.rem(x + 2, NX)], F.at[j], s_m.at[0], r_m1.at[j], to_f).start()
        rcopy(Pb.at[q, xb], RB.at[j], s_m.at[1], r_m2.at[j], to_b).start()

    GN[...] = lax.dot_general(
        G[...].reshape(256, 768), W[...].reshape(768, 768), (((1,), (1,)), ((), ())),
        preferred_element_type=F32,
    ).reshape(2, 128, 768)
    gn_send = rcopy(GN.at[1 - core], GNr, s_c.at[2], r_c.at[2], sib)
    gn_send.start()

    def forward_x(j, q):
        landed(F.at[j], r_m1.at[j])
        TB[j] = (F[j].astype(F32) + Pf[q, xf]).astype(BF16)
        rcopy(TB.at[j], RF.at[j], s_m.at[2], r_m3.at[j], to_f).start()

    def into_y(j, q):
        landed(RB.at[j], r_m2.at[j])
        landed(RF.at[j], r_m3.at[j])
        total = Pf[q, x] + RB[j].astype(F32) + RF[j].astype(F32)
        SXb[q] = total.astype(BF16)
        for d in (j, j + 4):
            if d:
                cols = pl.ds(pl.multiple_of(lax.div(lax.rem(y + d, NY), NYL) * 384, 128), 384)
                rcopy(SXb.at[q, :, cols], RY.at[d - 1], s_y, r_y, dxy(0, d)).start()
        if j == 0:
            SX[...] = total

    forward_x(*pieces[0])
    forward_x(*pieces[1])
    gn_send.wait_recv()

    def ln_back(h, carry):
        at = pl.ds(pl.multiple_of(h * 16, 16), 16)
        sums_g, sums_b = carry
        gn = [
            GN[core, at, ck * 128 : (ck + 1) * 128] + GNr[at, ck * 128 : (ck + 1) * 128]
            for ck in range(CH)
        ]
        wh = [cv[ck, h] for ck in range(CH)]
        sums_b = [a + g for a, g in zip(sums_b, gn)]
        sums_g = [a + g * w for a, g, w in zip(sums_g, gn, wh)]
        gw = [g * kT[ck, 49:50, :] for ck, g in enumerate(gn)]
        t1, t2 = gw[0], gw[0] * wh[0]
        for ck in range(1, CH):
            t1 = t1 + gw[ck]
            t2 = t2 + gw[ck] * wh[ck]
        m_1 = jnp.sum(t1, axis=-1, keepdims=True) * (1.0 / 768)
        m_2 = jnp.sum(t2, axis=-1, keepdims=True) * (1.0 / 768)
        inv = istd[h]
        for ck in range(CH):
            gp[ck, h, 8:24, :] = inv * (gw[ck] - m_1 - wh[ck] * m_2)
        return sums_g, sums_b

    zeros = [jnp.zeros((16, 128), F32) for _ in range(CH)]
    sums_g, sums_b = lax.fori_loop(0, 8, ln_back, (zeros, zeros))
    for ck in range(CH):
        K[ck, 49:50, :] = jnp.sum(sums_g[ck], axis=0, keepdims=True)
        K[ck, 50:51, :] = jnp.sum(sums_b[ck], axis=0, keepdims=True)
    forward_x(*pieces[2])
    forward_x(*pieces[3])

    def kernel_grad(ck):
        g = [gp[ck, h, 8:24, :] for h in range(8)]
        for b in range(KS):
            acc = [None] * KS
            for row in range(8):
                xs = xp[ck, row, pl.ds(5 + b, 16), :]
                for a in range(KS):
                    h = row - a + 3
                    if 0 <= h < 8:
                        t = xs * g[h]
                        acc[a] = t if acc[a] is None else acc[a] + t
            for a in range(KS):
                K[ck, a * KS + b : a * KS + b + 1, :] = jnp.sum(acc[a], axis=0, keepdims=True)

    pl.loop(0, CH // 2)(kernel_grad)
    into_y(*pieces[0])
    pl.loop(CH // 2, CH)(kernel_grad)

    for ck in range(CH):
        Kt[ck * 128 : (ck + 1) * 128, :] = jnp.transpose(K[ck])
    kt = Kt[...].reshape(16, 48, 128)
    kt = kt[:, :24] + pltpu.roll(kt[:, 24:].reshape(384, 128), 64, 1).reshape(16, 24, 128)
    Kf[...] = kt
    Kb[...] = kt.astype(BF16)
    for k in range(1, 16):
        qx, ql = lax.rem(x + k // 4, NX), lax.rem(yl + dy_of(k % 4) + NYL, NYL)
        rcopy(Kb.at[ql * QUAD + qx], RK.at[k - 1], s_k, r_k, dxy(k // 4, dy_of(k % 4))).start()

    for piece in pieces[1:]:
        into_y(*piece)

    landed(RK, r_k)
    ksum = Kf[slot]
    for k in range(15):
        ksum = ksum + RK[k].astype(F32)
    KS_[0:24, :] = ksum
    KS_[24:48, :] = pltpu.roll(ksum, 64, 1)
    landed(RY, r_y)
    ysum = SX[:, pl.ds(pl.multiple_of(yh * 384, 128), 384)]
    for d in range(NY - 1):
        ysum = ysum + RY[d].astype(F32)
    SY[...] = ysum
    for j in range(QUAD):
        ZSf[j, 0:12, 0:384] = SY[12 * j : 12 * j + 12, :]
        ZSf[j, 0:12, 384:512] = KS_[12 * j : 12 * j + 12, :]
    ZS[...] = ZSf[...].astype(BF16)
    for j in range(QUAD):
        @pl.when(x * QUAD + j != z)
        def _():
            rcopy(ZS.at[j], RZ.at[z], s_z2, r_z2, dev(x, y, x * QUAD + j, core)).start()

    @pl.loop(0, CH)
    def _(ck):
        acc = [jnp.zeros((16, 128), F32) for _ in range(8)]
        for b in range(KS):
            taps = [kT[ck, pl.ds(a * KS + b, 1), :] for a in range(KS)]
            for row in range(8):
                gs = gp[ck, row, pl.ds(11 - b, 16), :]
                for a in range(KS):
                    h = row + a - 3
                    if 0 <= h < 8:
                        acc[h] = acc[h] + gs * taps[a]
        lanes = pl.ds(pl.multiple_of(ck * 128, 128), 128)
        for h in range(8):
            gi_ref[h, :, lanes] = acc[h].astype(BF16)

    store = pltpu.make_async_copy(gi_ref, gi_hbm, s_in.at[4])
    store.start()

    p = yh * NC + core

    @pl.when(source)
    def _():
        RZ[z] = ZS[zr]
        landed(RZ.at[pl.ds(0, 15)], r_z2)
        total = RZ[0].astype(F32)
        for k in range(1, NZ):
            total = total + RZ[k].astype(F32)
        FIN[...] = total
        for i in range(1, NX):
            rcopy(FIN, PC.at[p], s_r1, r_r1, dxy(i, 0)).start()
        PC[p] = total

    @pl.when(jnp.logical_not(source))
    def _():
        landed(FIN, r_r1)

    for to in (sib, dxy(0, NYL), far):
        rcopy(PC.at[p], PC.at[p], s_r2, r_r2, to).start()
    landed(PC.at[pl.ds(0, 3)], r_r2)
    for q in range(4):
        at = (q % NC) * 768 + (q // NC) * 384
        gu_ref[:, at : at + 384] = PC[q, 0:12, 0:384]
    sm_ref[...] = (PC[0, 0:12, 384:] + PC[1, 0:12, 384:]) + (PC[2, 0:12, 384:] + PC[3, 0:12, 384:])

    @pl.when(source)
    def _():
        left(zall, s_z)
        left(PC.at[pl.ds(0, 3)], s_r1)
        left(ZS.at[pl.ds(0, 3)], s_z2)

    @pl.when(jnp.logical_not(source))
    def _():
        left(ZS, s_z2)

    store.wait()
    for c in (cot_send, n_send, gn_send):
        c.wait_send()
    left(S.at[pl.ds(0, 15)], s_g2)
    left(W.at[0, pl.ds(0, 3), :, A], s_w.at[0])
    left(W.at[0, pl.ds(0, 3), :, B], s_w.at[1])
    left(W.at[pl.ds(0, 3), :, :, A], s_w.at[2])
    left(W.at[pl.ds(0, 3), :, :, B], s_w.at[3])
    for i in range(3):
        left(TB, s_m.at[i])
    left(RY, s_y)
    left(RK, s_k)
    left(PC.at[pl.ds(0, 3)], s_r2)


def body(images, cotangent, depthwise_weight, norm_gain, norm_bias, up_weight):
    pixels = (
        images.shape[0] * images.shape[1] * images.shape[2]
        * lax.axis_size("shard") * lax.axis_size("rep")
    )
    factor = 1.0 / math.sqrt(pixels)
    dma = pltpu.SemaphoreType.DMA
    vm = lambda dtype, *shape: pltpu.VMEM(shape, dtype)
    gi, gu, sm = pl.pallas_call(
        kernel,
        out_shape=(
            jax.ShapeDtypeStruct((8, 16, 768), BF16),
            jax.ShapeDtypeStruct((12, 1536), F32),
            jax.ShapeDtypeStruct((12, 128), F32),
        ),
        in_specs=[pl.BlockSpec(memory_space=pltpu.HBM)] * 6,
        out_specs=[
            pl.BlockSpec(memory_space=pltpu.HBM),
            pl.BlockSpec(memory_space=pltpu.VMEM),
            pl.BlockSpec(memory_space=pltpu.VMEM),
        ],
        scratch_shapes=[
            vm(BF16, 8, 16, 768),
            vm(BF16, 8, 16, 768),
            vm(BF16, 12, 1536),
            vm(BF16, 12, 49),
            vm(BF16, 1, 12),
            vm(BF16, 1, 12),
            vm(F32, 16, 896),
            vm(BF16, 16, 896),
            vm(BF16, 15, 16, 896),
            vm(BF16, 4, 16, 896),
            vm(BF16, 4, 4, 48, 768),
            vm(BF16, 16, 24, 128),
            vm(F32, CH, 64, 128),
            vm(F32, CH, 8, 32, 128),
            vm(F32, CH, 8, 32, 128),
            vm(F32, CH, 8, 16, 128),
            vm(F32, 8, 16, 128),
            vm(BF16, 2, 128, 768),
            vm(BF16, 768, 256),
            vm(BF16, 2, 128, 768),
            vm(F32, 256, 768),
            vm(BF16, 2, 128, 768),
            vm(F32, 2, 128, 768),
            vm(F32, 128, 768),
            vm(F32, 4, 4, 48, 768),
            vm(BF16, 4, 4, 48, 768),
            vm(BF16, 4, 48, 768),
            vm(BF16, 4, 48, 768),
            vm(BF16, 4, 48, 768),
            vm(BF16, 4, 48, 768),
            vm(F32, 48, 768),
            vm(BF16, 4, 48, 768),
            vm(BF16, 7, 48, 384),
            vm(F32, 48, 384),
            vm(F32, CH, 128, 128),
            vm(F32, 768, 128),
            vm(F32, 16, 24, 128),
            vm(BF16, 16, 24, 128),
            vm(BF16, 15, 24, 128),
            vm(F32, 48, 128),
            vm(F32, 4, 16, 512),
            vm(BF16, 4, 16, 512),
            vm(BF16, 16, 16, 512),
            vm(F32, 16, 512),
            vm(F32, 4, 16, 512),
            dma((6,)),
            dma, dma,
            dma, dma,
            dma((4,)), dma((4,)),
            dma((3,)), dma((3,)),
            dma((3,)), dma((4,)), dma((4,)), dma((4,)),
            dma, dma,
            dma, dma,
            dma, dma,
            dma, dma,
            dma, dma,
        ],
        compiler_params=pltpu.CompilerParams(
            collective_id=0, has_side_effects=True, vmem_limit_bytes=58 << 20
        ),
    )(
        images.reshape(8, 16, 768), cotangent.reshape(128, 1536), depthwise_weight,
        norm_gain.reshape(1, 12), norm_bias.reshape(1, 12), up_weight,
    )
    taps = KS * KS
    sm = sm * factor
    return (gi.reshape(images.shape), gu * factor, sm[:, :taps], sm[:, taps], sm[:, taps + 1])


def solution(mesh):
    placed = (
        P(("shard", "rep"), None, None, None),
        P(("shard", "rep"), None, None, None),
        P("shard", None),
        P("shard"),
        P("shard"),
        P("shard", None),
    )
    return jax.shard_map(
        body,
        mesh=mesh,
        in_specs=placed,
        out_specs=(
            P(("shard", "rep"), None, None, None),
            P("shard", None),
            P("shard", None),
            P("shard"),
            P("shard"),
        ),
        check_vma=False,
    )
```

time: 108 us -> 96.4 us (0.89)
  Pallas kernels: 99.4 us -> 91.7 us
  local copies, waits for them, and re-layouts: 7.48 us -> 1.38 us
  other arithmetic: 0.02 us -> 2.28 us
    pallas_call x1, Pallas kernels: 99.4 us -> 91.7 us  [body(): pl.pallas_call(kernel, out_shape=(jax.ShapeDtypeStruct((8, 16, 768), BF16...]
    mul x0 -> x2, other arithmetic: none -> 2.28 us  [the longest x1 1.54 us: body(): gu * factor]
    unnamed x7 -> x5, local copies, waits for them, and re-layouts: 2.91 us -> 0.68 us
    concatenate x2 -> x0, local copies, waits for them, and re-layouts: 1.55 us -> none  [the longest x1 0.78 us: body(): jnp.concatenate([up_weight[:, :768], small], 1)]
    broadcast_in_dim x3 -> x0, local copies, waits for them, and re-layouts: 1.54 us -> none  [the longest x1 0.78 us: body(): norm_gain[:, None]]
where the time goes in v2:
time: 96.4 us; the launch traced here: 96 us
  Pallas kernels  91.7 us (95%)
  other arithmetic  2.28 us (2%)
  local copies, waits for them, and re-layouts  1.38 us (1%)
    pallas_call x1, Pallas kernels, body(): pl.pallas_call(kernel, out_shape=(jax.ShapeDtypeStruct((8, 16, 768), BF16...  91.7 us

profile of v2, /device:TPU:5, one launch (start us, length us, event | category | flops | bytes accessed | tf_op | source)
XLA Modules:
  0.0 96.0 jit_solution(17419674610724406285)
XLA Ops:
  0.6 91.7 %shard_map.101 = (bf16[8,16,768]{2,1,0:T(8,128)(2,1)}, f32[12,1536]{1,0:T(8,128)}, f32[12,128]{1,0:T(8,128)}) custom-call(bf16[8,16,768]{2,1,0:T(8,128)(2,1)} %bitcast.8, bf16[128,1536]{1,0:T(8,128)(2,1)} %bitcast.6, bf16[12,49]{1,0:T(8,128)(2,1)} %dw_hbm.1, bf16[1,12]{1,0:T(2,128)(2,1)} %bitcast.10, bf16[1,12]{1,0:T(2,128)(2,1)} %bitcast.11, ...), custom_call_target="tpu_custom_call" | custom-call | tf_op jit(solution)/shard_map/pallas_call | solution.py:451
  92.4 0.0 copy-start
  92.4 0.7 broadcast_multiply_fusion.1
  93.1 0.0 copy-start.1
  93.1 0.7 slice_reduce_fusion
  93.8 0.0 copy-done.1
  93.8 1.5 %broadcast_multiply_fusion = f32[12,1536]{1,0:T(8,128)} fusion(f32[12,1536]{1,0:T(8,128)} %get-tuple-element.9), kind=kLoop, calls=%fused_computation | loop fusion | flops 18432 | bytes 147456 | tf_op jit(solution)/shard_map/mul | solution.py:531
  95.4 0.0 copy-done
  95.4 0.7 copy.12
Async XLA Ops:
  92.4 3.0 %copy-start = (bf16[8,16,768]{2,1,0:T(8,128)(2,1)S(1)}, bf16[8,16,768]{2,1,0:T(8,128)(2,1)}, u32[]{:S(2)}) copy-start(bf16[8,16,768]{2,1,0:T(8,128)(2,1)} %get-tuple-element.8) | copy-start | bytes 589828
  93.1 0.7 copy-start.1

commit v3 on v2

--- a/solution.py
+++ b/solution.py
@@ -26,8 +26,8 @@
 
 def kernel(
     img_hbm, cot_hbm, dw_hbm, gain_hbm, bias_hbm, up_hbm,
-    gi_hbm, gu_ref, sm_ref,
-    gi_ref, imgv, upv, dwv, gnv, bsv, wlf, wl, zall,
+    gi_ref, gu_ref, sm_ref,
+    gip, order, imgv, upv, dwv, gnv, bsv, wlf, wl, zall,
     zbuf, W, S, kT, xp, gp, cv, istd, N, NT, Ct, pre, G, GN, GNr,
     Pf, Pb, F, RB, RF, TB, SX, SXb, RY, SY, K, Kt, Kf, Kb, RK, KS_, ZSf, ZS, RZ, FIN, PC,
     s_in, s_z, r_z, s_g2, r_g2, s_w, r_w, s_c, r_c,
@@ -41,8 +41,8 @@
     core = lax.rem(r, NC)
     y = yh * NYL + yl
     sgn = 1 - 2 * core
-    zq, zr = lax.div(z, QUAD), lax.rem(z, QUAD)
-    source = zq == x
+    zr = lax.div(z, QUAD)
+    source = lax.rem(z, QUAD) == x
 
     def dev(x_, y_, z_, c_):
         return (
@@ -53,6 +53,9 @@
     def dz(k):
         return dev(x, y, lax.rem(z + k, NZ), core)
 
+    def far_first(i):
+        return 8 + lax.div(i + 1, 2) * (1 - 2 * lax.rem(i, 2))
+
     def dxy(dx, dy):
         return dev(lax.rem(x + dx + 2 * NX, NX), lax.rem(y + dy + 2 * NY, NY), z, core)
 
@@ -83,14 +86,14 @@
 
     @pl.when(source)
     def _():
-        @pl.loop(1, NZ)
-        def _(k):
-            hello(dz(k))
+        @pl.loop(0, NZ - 1)
+        def _(i):
+            hello(dz(far_first(i)))
 
     @pl.when(jnp.logical_not(source))
     def _():
         for j in range(QUAD):
-            hello(dev(x, y, x * QUAD + j, core))
+            hello(dev(x, y, x + QUAD * j, core))
 
     loads = [
         pltpu.make_async_copy(src, dst, s_in.at[i])
@@ -128,9 +131,9 @@
 
     @pl.when(source)
     def _():
-        @pl.loop(1, NZ)
-        def _(k):
-            rcopy(wl, zbuf.at[zr], s_z, r_z, dz(k)).start()
+        @pl.loop(0, NZ - 1)
+        def _(i):
+            rcopy(wl, zbuf.at[zr], s_z, r_z, dz(far_first(i))).start()
 
         zbuf[zr] = wl[...]
 
@@ -138,13 +141,26 @@
     cot_send.start()
 
     zero_edge = jnp.zeros((8, 8, 128), F32)
+    place = lax.broadcasted_iota(jnp.int32, (8, 768), 1)
+    block, inner = place // 48, place % 48
+    channel = (block // QUAD * NZ + block % QUAD + QUAD * (inner // 12)) * 12 + inner % 12
+    near = lax.broadcasted_iota(jnp.int32, (8, 768), 0)
+
+    @pl.loop(0, 48)
+    def _(i):
+        at = pl.multiple_of(i * 16, 16)
+        order[pl.ds(at, 16), :] = jnp.concatenate(
+            [jnp.where(channel == near + (at + h), 1.0, 0.0) for h in (0, 8)], axis=0
+        ).astype(BF16)
+
     loads[4].wait()
+    image = jnp.dot(imgv[...].reshape(128, 768), order[...], preferred_element_type=F32)
     for ck in range(CH):
         xp[ck, :, 0:8, :] = zero_edge
         xp[ck, :, 24:32, :] = zero_edge
         gp[ck, :, 0:8, :] = zero_edge
         gp[ck, :, 24:32, :] = zero_edge
-        xp[ck, :, 8:24, :] = imgv[:, :, ck * 128 : (ck + 1) * 128].astype(F32)
+        xp[ck, :, 8:24, :] = image[:, ck * 128 : (ck + 1) * 128].reshape(8, 16, 128)
     K[...] = jnp.zeros_like(K)
     ZSf[...] = jnp.zeros_like(ZSf)
     loads[5].wait()
@@ -251,7 +267,7 @@
     xf = lax.rem(x + sgn + NX, NX)
     xb = lax.rem(x - sgn + NX, NX)
     to_f, to_b = dxy(sgn, 0), dxy(-sgn, 0)
-    pieces = [(j, lax.rem(yl + j, NYL)) for j in (2, 3, 1, 0)]
+    pieces = [(j, lax.rem(yl + j, NYL)) for j in (0, 1, 3, 2)]
     for j, q in pieces:
         part = jnp.dot(
             NT[pl.ds(pl.multiple_of(q * 192, 64), 192), :], G[...].reshape(256, 768),
@@ -287,7 +303,6 @@
             SX[...] = total
 
     forward_x(*pieces[0])
-    forward_x(*pieces[1])
     gn_send.wait_recv()
 
     def ln_back(h, carry):
@@ -317,8 +332,7 @@
     for ck in range(CH):
         K[ck, 49:50, :] = jnp.sum(sums_g[ck], axis=0, keepdims=True)
         K[ck, 50:51, :] = jnp.sum(sums_b[ck], axis=0, keepdims=True)
-    forward_x(*pieces[2])
-    forward_x(*pieces[3])
+    forward_x(*pieces[1])
 
     def kernel_grad(ck):
         g = [gp[ck, h, 8:24, :] for h in range(8)]
@@ -335,8 +349,9 @@
                 K[ck, a * KS + b : a * KS + b + 1, :] = jnp.sum(acc[a], axis=0, keepdims=True)
 
     pl.loop(0, CH // 2)(kernel_grad)
-    into_y(*pieces[0])
+    forward_x(*pieces[2])
     pl.loop(CH // 2, CH)(kernel_grad)
+    forward_x(*pieces[3])
 
     for ck in range(CH):
         Kt[ck * 128 : (ck + 1) * 128, :] = jnp.transpose(K[ck])
@@ -348,7 +363,7 @@
         qx, ql = lax.rem(x + k // 4, NX), lax.rem(yl + dy_of(k % 4) + NYL, NYL)
         rcopy(Kb.at[ql * QUAD + qx], RK.at[k - 1], s_k, r_k, dxy(k // 4, dy_of(k % 4))).start()
 
-    for piece in pieces[1:]:
+    for piece in pieces:
         into_y(*piece)
 
     landed(RK, r_k)
@@ -367,9 +382,9 @@
         ZSf[j, 0:12, 384:512] = KS_[12 * j : 12 * j + 12, :]
     ZS[...] = ZSf[...].astype(BF16)
     for j in range(QUAD):
-        @pl.when(x * QUAD + j != z)
+        @pl.when(x + QUAD * j != z)
         def _():
-            rcopy(ZS.at[j], RZ.at[z], s_z2, r_z2, dev(x, y, x * QUAD + j, core)).start()
+            rcopy(ZS.at[j], RZ.at[z], s_z2, r_z2, dev(x, y, x + QUAD * j, core)).start()
 
     @pl.loop(0, CH)
     def _(ck):
@@ -384,10 +399,11 @@
                         acc[h] = acc[h] + gs * taps[a]
         lanes = pl.ds(pl.multiple_of(ck * 128, 128), 128)
         for h in range(8):
-            gi_ref[h, :, lanes] = acc[h].astype(BF16)
-
-    store = pltpu.make_async_copy(gi_ref, gi_hbm, s_in.at[4])
-    store.start()
+            gip[h, :, lanes] = acc[h].astype(BF16)
+
+    gi_ref[...] = lax.dot_general(
+        gip[...].reshape(128, 768), order[...], (((1,), (1,)), ((), ())), preferred_element_type=F32
+    ).reshape(8, 16, 768).astype(BF16)
 
     p = yh * NC + core
 
@@ -425,7 +441,6 @@
     def _():
         left(ZS, s_z2)
 
-    store.wait()
     for c in (cot_send, n_send, gn_send):
         c.wait_send()
     left(S.at[pl.ds(0, 15)], s_g2)
@@ -456,13 +471,10 @@
             jax.ShapeDtypeStruct((12, 128), F32),
         ),
         in_specs=[pl.BlockSpec(memory_space=pltpu.HBM)] * 6,
-        out_specs=[
-            pl.BlockSpec(memory_space=pltpu.HBM),
-            pl.BlockSpec(memory_space=pltpu.VMEM),
-            pl.BlockSpec(memory_space=pltpu.VMEM),
-        ],
+        out_specs=[pl.BlockSpec(memory_space=pltpu.VMEM)] * 3,
         scratch_shapes=[
             vm(BF16, 8, 16, 768),
+            vm(BF16, 768, 768),
             vm(BF16, 8, 16, 768),
             vm(BF16, 12, 1536),
             vm(BF16, 12, 49),
@@ -520,11 +532,16 @@
             dma, dma,
         ],
         compiler_params=pltpu.CompilerParams(
-            collective_id=0, has_side_effects=True, vmem_limit_bytes=58 << 20
+            collective_id=0, has_side_effects=True, vmem_limit_bytes=40 << 20
         ),
     )(
-        images.reshape(8, 16, 768), cotangent.reshape(128, 1536), depthwise_weight,
-        norm_gain.reshape(1, 12), norm_bias.reshape(1, 12), up_weight,
+        *[
+            pltpu.with_memory_space_constraint(v, pltpu.HBM)
+            for v in (
+                images.reshape(8, 16, 768), cotangent.reshape(128, 1536), depthwise_weight,
+                norm_gain.reshape(1, 12), norm_bias.reshape(1, 12), up_weight,
+            )
+        ]
     )
     taps = KS * KS
     sm = sm * factor

time: 96.4 us -> 83.6 us (0.87)
  Pallas kernels: 91.7 us -> 80.8 us
  other arithmetic: 2.28 us -> 0.65 us
    pallas_call x1, Pallas kernels: 91.7 us -> 80.8 us  [body(): pl.pallas_call(kernel, out_shape=(jax.ShapeDtypeStruct((8, 16, 768), BF16...]
where the time goes in v3:
time: 83.6 us; the launch traced here: 83.5 us
  Pallas kernels  80.8 us (97%)
  local copies, waits for them, and re-layouts  1.38 us (2%)
    pallas_call x1, Pallas kernels, body(): pl.pallas_call(kernel, out_shape=(jax.ShapeDtypeStruct((8, 16, 768), BF16...  80.8 us

profile of v3, /device:TPU:5, one launch (start us, length us, event | category | flops | bytes accessed | tf_op | source)
XLA Modules:
  0.0 83.5 jit_solution(2437110894733485053)
XLA Ops:
  0.6 80.8 %shard_map.101 = (bf16[8,16,768]{2,1,0:T(8,128)(2,1)S(1)}, f32[12,1536]{1,0:T(8,128)S(1)}, f32[12,128]{1,0:T(8,128)S(1)}) custom-call(bf16[8,16,768]{2,1,0:T(8,128)(2,1)} %bitcast.8, bf16[128,1536]{1,0:T(8,128)(2,1)} %bitcast.7, bf16[12,49]{1,0:T(8,128)(2,1)} %dw_hbm.1, bf16[1,12]{1,0:T(2,128)(2,1)} %bitcast.10, bf16[1,12]{1,0:T(2,128)(2,1)} %bitcast.11, ...), custom_call_target="tpu_custom_call" | custom-call | tf_op jit(solution)/shard_map/pallas_call | solution.py:466
  81.4 0.0 copy-start
  81.4 0.7 slice_reduce_fusion
  82.1 0.0 copy-done
  82.1 0.7 broadcast_multiply_fusion
  82.8 0.7 copy.12
  (1 shorter events, 0.0 us)
Async XLA Ops:
  81.4 0.7 copy-start

commit v4 on v3

--- a/solution.py
+++ b/solution.py
@@ -17,6 +17,7 @@
 NY = NYL * NYH
 QUAD = 4
 CH = 6
+FAR_FIRST = sorted(range(1, NZ), key=lambda k: abs(k - NZ // 2))
 
 
 def gelu_slope(v):
@@ -27,9 +28,9 @@
 def kernel(
     img_hbm, cot_hbm, dw_hbm, gain_hbm, bias_hbm, up_hbm,
     gi_ref, gu_ref, sm_ref,
-    gip, order, imgv, upv, dwv, gnv, bsv, wlf, wl, zall,
+    gip, order, imgv, upv, dwv, gnv, bsv, wlf, sml, wl, zall,
     zbuf, W, S, kT, xp, gp, cv, istd, N, NT, Ct, pre, G, GN, GNr,
-    Pf, Pb, F, RB, RF, TB, SX, SXb, RY, SY, K, Kt, Kf, Kb, RK, KS_, ZSf, ZS, RZ, FIN, PC,
+    Pf, Pb, F, RB, RF, TB, SX, SXb, RY, SY, K, Kt, Kf, Kb, RK, KS_, ZSf, ZS, RZ, FIN, PH, PC,
     s_in, s_z, r_z, s_g2, r_g2, s_w, r_w, s_c, r_c,
     s_m, r_m1, r_m2, r_m3, s_y, r_y, s_k, r_k, s_z2, r_z2, s_r1, r_r1, s_r2, r_r2,
 ):
@@ -53,14 +54,10 @@
     def dz(k):
         return dev(x, y, lax.rem(z + k, NZ), core)
 
-    def far_first(i):
-        return 8 + lax.div(i + 1, 2) * (1 - 2 * lax.rem(i, 2))
-
     def dxy(dx, dy):
         return dev(lax.rem(x + dx + 2 * NX, NX), lax.rem(y + dy + 2 * NY, NY), z, core)
 
     sib = dev(x, y, z, 1 - core)
-    far = dev(x, lax.rem(y + NYL, NY), z, 1 - core)
 
     def rcopy(src, dst, ss, rs, to):
         return pltpu.make_async_remote_copy(
@@ -86,9 +83,8 @@
 
     @pl.when(source)
     def _():
-        @pl.loop(0, NZ - 1)
-        def _(i):
-            hello(dz(far_first(i)))
+        for k in FAR_FIRST:
+            hello(dz(k))
 
     @pl.when(jnp.logical_not(source))
     def _():
@@ -110,13 +106,15 @@
         for i in range(4):
             hello(dxy(-dx, -dy_of(i)))
     hello(sib)
-    hello(far)
+    for dy in (2, NY - 2):
+        hello(dev(x, lax.rem(y + dy, NY), z, 1 - core))
 
     wlf[...] = jnp.zeros_like(wlf)
     for c in loads[:4]:
         c.wait()
     wlf[0:12, 0:768] = upv[:, half_own].astype(F32)
-    wlf[0:12, 768:817] = dwv[...].astype(F32)
+    sml[...] = jnp.zeros_like(sml)
+    sml[:, 0:49] = dwv[...].astype(F32)
     row12 = lax.broadcasted_iota(jnp.int32, (12, 12), 0)
     col12 = lax.broadcasted_iota(jnp.int32, (12, 12), 1)
 
@@ -125,15 +123,16 @@
 
     lane = lax.broadcasted_iota(jnp.int32, (12, 128), 1)
     extra = jnp.where(lane == 49, column(gnv), jnp.where(lane == 50, column(bsv), 0.0))
-    wlf[0:12, 768:896] = wlf[0:12, 768:896] + extra
+    sml[...] = sml[...] + extra
+    for t in range(3):
+        wlf[12:16, t * 128 : (t + 1) * 128] = sml[4 * t : 4 * t + 4, :]
     wl[...] = wlf[...].astype(BF16)
-    pl.semaphore_wait(barrier, 25 + 11 * source.astype(jnp.int32))
+    pl.semaphore_wait(barrier, 26 + 11 * source.astype(jnp.int32))
 
     @pl.when(source)
     def _():
-        @pl.loop(0, NZ - 1)
-        def _(i):
-            rcopy(wl, zbuf.at[zr], s_z, r_z, dz(far_first(i))).start()
+        for k in FAR_FIRST:
+            rcopy(wl, zbuf.at[zr], s_z, r_z, dz(k)).start()
 
         zbuf[zr] = wl[...]
 
@@ -162,7 +161,6 @@
         gp[ck, :, 24:32, :] = zero_edge
         xp[ck, :, 8:24, :] = image[:, ck * 128 : (ck + 1) * 128].reshape(8, 16, 128)
     K[...] = jnp.zeros_like(K)
-    ZSf[...] = jnp.zeros_like(ZSf)
     loads[5].wait()
 
     @pl.when(source)
@@ -176,17 +174,24 @@
     rows = lax.broadcasted_iota(jnp.int32, (48, 64), 0)
     cols = lax.broadcasted_iota(jnp.int32, (48, 64), 1)
     pick48 = jnp.where(rows // 12 * 16 + rows % 12 == cols, 1.0, 0.0).astype(BF16)
-    packed = jnp.dot(pick48, zbuf[...].reshape(64, 896), preferred_element_type=F32)
-    W[yl, x] = packed[:, :768].astype(BF16)
+    blocks = zbuf[...].reshape(64, 768)
+    W[yl, x] = jnp.dot(pick48, blocks, preferred_element_type=F32).astype(BF16)
+    small = jnp.zeros((48, 128), F32)
+    for t in range(3):
+        here = jnp.logical_and(rows % 12 // 4 == t, rows // 12 * 16 + 12 + rows % 4 == cols)
+        small = small + jnp.dot(
+            jnp.where(here, 1.0, 0.0).astype(BF16), blocks[:, t * 128 : (t + 1) * 128],
+            preferred_element_type=F32,
+        )
     slot = yl * QUAD + x
-    S[slot] = (packed[0:24, 768:] + pltpu.roll(packed[24:48, 768:], 64, 1)).astype(BF16)
-
-    for k in range(1, 16):
-        rcopy(S.at[slot], S.at[slot], s_g2, r_g2, dxy(k // 4, dy_of(k % 4))).start()
+    S[slot] = (small[0:24] + pltpu.roll(small[24:48], 64, 1)).astype(BF16)
+
     A, B = pl.ds(0, 384), pl.ds(384, 384)
     for i in range(1, 4):
         rcopy(W.at[yl, x, :, A], W.at[yl, x, :, A], s_w.at[0], r_w.at[0], dxy(0, dy_of(i))).start()
         rcopy(W.at[yl, x, :, B], W.at[yl, x, :, B], s_w.at[1], r_w.at[1], dxy(i, 0)).start()
+    for k in range(1, 16):
+        rcopy(S.at[slot], S.at[slot], s_g2, r_g2, dxy(k // 4, dy_of(k % 4))).start()
 
     landed(W.at[0, pl.ds(0, 3), :, A], r_w.at[0])
     for i in range(1, 4):
@@ -267,7 +272,7 @@
     xf = lax.rem(x + sgn + NX, NX)
     xb = lax.rem(x - sgn + NX, NX)
     to_f, to_b = dxy(sgn, 0), dxy(-sgn, 0)
-    pieces = [(j, lax.rem(yl + j, NYL)) for j in (0, 1, 3, 2)]
+    pieces = [(j, lax.rem(yl + j, NYL)) for j in (2, 3, 1, 0)]
     for j, q in pieces:
         part = jnp.dot(
             NT[pl.ds(pl.multiple_of(q * 192, 64), 192), :], G[...].reshape(256, 768),
@@ -295,11 +300,11 @@
         landed(RF.at[j], r_m3.at[j])
         total = Pf[q, x] + RB[j].astype(F32) + RF[j].astype(F32)
         SXb[q] = total.astype(BF16)
-        for d in (j, j + 4):
+        for d in ((j + 2) % 4, (j + 2) % 4 + 4):
             if d:
                 cols = pl.ds(pl.multiple_of(lax.div(lax.rem(y + d, NY), NYL) * 384, 128), 384)
                 rcopy(SXb.at[q, :, cols], RY.at[d - 1], s_y, r_y, dxy(0, d)).start()
-        if j == 0:
+        if j == 2:
             SX[...] = total
 
     forward_x(*pieces[0])
@@ -360,14 +365,14 @@
     Kf[...] = kt
     Kb[...] = kt.astype(BF16)
     for k in range(1, 16):
-        qx, ql = lax.rem(x + k // 4, NX), lax.rem(yl + dy_of(k % 4) + NYL, NYL)
+        qx, ql = lax.rem(x + k // 4, NX), lax.rem(yl + dy_of(k % 4) + 2 + NYL, NYL)
         rcopy(Kb.at[ql * QUAD + qx], RK.at[k - 1], s_k, r_k, dxy(k // 4, dy_of(k % 4))).start()
 
     for piece in pieces:
         into_y(*piece)
 
     landed(RK, r_k)
-    ksum = Kf[slot]
+    ksum = Kf[lax.rem(yl + 2, NYL) * QUAD + x]
     for k in range(15):
         ksum = ksum + RK[k].astype(F32)
     KS_[0:24, :] = ksum
@@ -378,8 +383,9 @@
         ysum = ysum + RY[d].astype(F32)
     SY[...] = ysum
     for j in range(QUAD):
-        ZSf[j, 0:12, 0:384] = SY[12 * j : 12 * j + 12, :]
-        ZSf[j, 0:12, 384:512] = KS_[12 * j : 12 * j + 12, :]
+        ZSf[j, 0:12, :] = SY[12 * j : 12 * j + 12, :]
+        for t in range(3):
+            ZSf[j, 12:16, t * 128 : (t + 1) * 128] = KS_[12 * j + 4 * t : 12 * j + 4 * t + 4, :]
     ZS[...] = ZSf[...].astype(BF16)
     for j in range(QUAD):
         @pl.when(x + QUAD * j != z)
@@ -414,22 +420,27 @@
         total = RZ[0].astype(F32)
         for k in range(1, NZ):
             total = total + RZ[k].astype(F32)
-        FIN[...] = total
+        FIN[...] = total.astype(BF16)
         for i in range(1, NX):
-            rcopy(FIN, PC.at[p], s_r1, r_r1, dxy(i, 0)).start()
-        PC[p] = total
+            rcopy(FIN, PH, s_r1, r_r1, dxy(i, 0)).start()
+        PH[...] = total.astype(BF16)
 
     @pl.when(jnp.logical_not(source))
     def _():
         landed(FIN, r_r1)
 
-    for to in (sib, dxy(0, NYL), far):
-        rcopy(PC.at[p], PC.at[p], s_r2, r_r2, to).start()
-    landed(PC.at[pl.ds(0, 3)], r_r2)
+    for dy in (2, NY - 2):
+        for c in (core, 1 - core):
+            rcopy(PH, PC.at[p], s_r2, r_r2, dev(x, lax.rem(y + dy, NY), z, c)).start()
+    landed(PC, r_r2)
     for q in range(4):
         at = (q % NC) * 768 + (q // NC) * 384
-        gu_ref[:, at : at + 384] = PC[q, 0:12, 0:384]
-    sm_ref[...] = (PC[0, 0:12, 384:] + PC[1, 0:12, 384:]) + (PC[2, 0:12, 384:] + PC[3, 0:12, 384:])
+        gu_ref[:, at : at + 384] = PC[q].astype(F32)[0:12]
+    spare = PC[0].astype(F32)[8:16]
+    for q in range(1, 4):
+        spare = spare + PC[q].astype(F32)[8:16]
+    for t in range(3):
+        sm_ref[4 * t : 4 * t + 4, :] = spare[4:8, t * 128 : (t + 1) * 128]
 
     @pl.when(source)
     def _():
@@ -452,7 +463,7 @@
         left(TB, s_m.at[i])
     left(RY, s_y)
     left(RK, s_k)
-    left(PC.at[pl.ds(0, 3)], s_r2)
+    left(PC, s_r2)
 
 
 def body(images, cotangent, depthwise_weight, norm_gain, norm_bias, up_weight):
@@ -480,10 +491,11 @@
             vm(BF16, 12, 49),
             vm(BF16, 1, 12),
             vm(BF16, 1, 12),
-            vm(F32, 16, 896),
-            vm(BF16, 16, 896),
-            vm(BF16, 15, 16, 896),
-            vm(BF16, 4, 16, 896),
+            vm(F32, 16, 768),
+            vm(F32, 12, 128),
+            vm(BF16, 16, 768),
+            vm(BF16, 15, 16, 768),
+            vm(BF16, 4, 16, 768),
             vm(BF16, 4, 4, 48, 768),
             vm(BF16, 16, 24, 128),
             vm(F32, CH, 64, 128),
@@ -514,11 +526,12 @@
             vm(BF16, 16, 24, 128),
             vm(BF16, 15, 24, 128),
             vm(F32, 48, 128),
-            vm(F32, 4, 16, 512),
-            vm(BF16, 4, 16, 512),
-            vm(BF16, 16, 16, 512),
-            vm(F32, 16, 512),
-            vm(F32, 4, 16, 512),
+            vm(F32, 4, 16, 384),
+            vm(BF16, 4, 16, 384),
+            vm(BF16, 16, 16, 384),
+            vm(BF16, 16, 384),
+            vm(BF16, 16, 384),
+            vm(BF16, 4, 16, 384),
             dma((6,)),
             dma, dma,
             dma, dma,

time: 83.6 us -> 80.6 us (0.964)
  Pallas kernels: 80.8 us -> 77.7 us
    pallas_call x1, Pallas kernels: 80.8 us -> 77.7 us  [body(): pl.pallas_call(kernel, out_shape=(jax.ShapeDtypeStruct((8, 16, 768), BF16...]
where the time goes in v4:
time: 80.6 us; the launch traced here: 80.4 us
  Pallas kernels  77.7 us (96%)
  local copies, waits for them, and re-layouts  1.38 us (2%)
    pallas_call x1, Pallas kernels, body(): pl.pallas_call(kernel, out_shape=(jax.ShapeDtypeStruct((8, 16, 768), BF16...  77.7 us

profile of v4, /device:TPU:5, one launch (start us, length us, event | category | flops | bytes accessed | tf_op | source)
XLA Modules:
  0.0 80.4 jit_solution(17251392993591674068)
XLA Ops:
  0.6 77.7 %shard_map.101 = (bf16[8,16,768]{2,1,0:T(8,128)(2,1)S(1)}, f32[12,1536]{1,0:T(8,128)S(1)}, f32[12,128]{1,0:T(8,128)S(1)}) custom-call(bf16[8,16,768]{2,1,0:T(8,128)(2,1)} %bitcast.8, bf16[128,1536]{1,0:T(8,128)(2,1)} %bitcast.7, bf16[12,49]{1,0:T(8,128)(2,1)} %dw_hbm.1, bf16[1,12]{1,0:T(2,128)(2,1)} %bitcast.10, bf16[1,12]{1,0:T(2,128)(2,1)} %bitcast.11, ...), custom_call_target="tpu_custom_call" | custom-call | tf_op jit(solution)/shard_map/pallas_call | solution.py:477
  78.4 0.0 copy-start
  78.4 0.7 slice_reduce_fusion
  79.1 0.0 copy-done
  79.1 0.7 broadcast_multiply_fusion
  79.7 0.7 copy.12
  (1 shorter events, 0.0 us)
Async XLA Ops:
  78.4 0.7 copy-start

commit v5 on v4

--- a/solution.py
+++ b/solution.py
@@ -1,3 +1,4 @@
+import functools
 import math
 
 import jax
@@ -25,9 +26,19 @@
     return cumulative + v * jnp.exp(-0.5 * v * v) * 0.3989422804014327
 
 
+def hand_over(*refs):
+    n = len(refs) // 2
+    copies = [pltpu.make_async_copy(refs[i], refs[n + i], refs[-1].at[i]) for i in range(n)]
+    for c in copies:
+        c.start()
+    for c in copies:
+        c.wait()
+
+
 def kernel(
+    factor,
     img_hbm, cot_hbm, dw_hbm, gain_hbm, bias_hbm, up_hbm,
-    gi_ref, gu_ref, sm_ref,
+    gi_ref, gu_ref, gd_ref, gg_ref, gb_ref,
     gip, order, imgv, upv, dwv, gnv, bsv, wlf, sml, wl, zall,
     zbuf, W, S, kT, xp, gp, cv, istd, N, NT, Ct, pre, G, GN, GNr,
     Pf, Pb, F, RB, RF, TB, SX, SXb, RY, SY, K, Kt, Kf, Kb, RK, KS_, ZSf, ZS, RZ, FIN, PH, PC,
@@ -435,12 +446,20 @@
     landed(PC, r_r2)
     for q in range(4):
         at = (q % NC) * 768 + (q // NC) * 384
-        gu_ref[:, at : at + 384] = PC[q].astype(F32)[0:12]
+        gu_ref[:, at : at + 384] = PC[q].astype(F32)[0:12] * factor
     spare = PC[0].astype(F32)[8:16]
     for q in range(1, 4):
         spare = spare + PC[q].astype(F32)[8:16]
     for t in range(3):
-        sm_ref[4 * t : 4 * t + 4, :] = spare[4:8, t * 128 : (t + 1) * 128]
+        sml[4 * t : 4 * t + 4, :] = spare[4:8, t * 128 : (t + 1) * 128] * factor
+    gd_ref[...] = sml[:, 0:49]
+
+    def across(t):
+        picked = jnp.sum(jnp.where(lane == t, sml[...], 0.0), axis=1, keepdims=True)
+        return jnp.sum(jnp.where(row12 == col12, picked, 0.0), axis=0, keepdims=True)
+
+    gg_ref[...] = across(49)
+    gb_ref[...] = across(50)
 
     @pl.when(source)
     def _():
@@ -474,15 +493,18 @@
     factor = 1.0 / math.sqrt(pixels)
     dma = pltpu.SemaphoreType.DMA
     vm = lambda dtype, *shape: pltpu.VMEM(shape, dtype)
-    gi, gu, sm = pl.pallas_call(
-        kernel,
-        out_shape=(
-            jax.ShapeDtypeStruct((8, 16, 768), BF16),
-            jax.ShapeDtypeStruct((12, 1536), F32),
-            jax.ShapeDtypeStruct((12, 128), F32),
-        ),
+    shapes = (
+        jax.ShapeDtypeStruct((8, 16, 768), BF16),
+        jax.ShapeDtypeStruct((12, 1536), F32),
+        jax.ShapeDtypeStruct((12, 49), F32),
+        jax.ShapeDtypeStruct((1, 12), F32),
+        jax.ShapeDtypeStruct((1, 12), F32),
+    )
+    results = pl.pallas_call(
+        functools.partial(kernel, factor),
+        out_shape=shapes,
         in_specs=[pl.BlockSpec(memory_space=pltpu.HBM)] * 6,
-        out_specs=[pl.BlockSpec(memory_space=pltpu.VMEM)] * 3,
+        out_specs=[pl.BlockSpec(memory_space=pltpu.VMEM)] * 5,
         scratch_shapes=[
             vm(BF16, 8, 16, 768),
             vm(BF16, 768, 768),
@@ -556,9 +578,15 @@
             )
         ]
     )
-    taps = KS * KS
-    sm = sm * factor
-    return (gi.reshape(images.shape), gu * factor, sm[:, :taps], sm[:, taps], sm[:, taps + 1])
+    gi, gu, gd, gg, gb = pl.pallas_call(
+        hand_over,
+        out_shape=shapes,
+        in_specs=[pl.BlockSpec(memory_space=pl.ANY)] * 5,
+        out_specs=[pl.BlockSpec(memory_space=pltpu.HBM)] * 5,
+        scratch_shapes=[dma((5,))],
+        compiler_params=pltpu.CompilerParams(vmem_limit_bytes=1 << 20),
+    )(*results)
+    return (gi.reshape(images.shape), gu, gd, gg.reshape(12), gb.reshape(12))
 
 
 def solution(mesh):

time: 80.6 us -> 79.4 us (0.985)
  local copies, waits for them, and re-layouts: 1.38 us -> 0 us
  Pallas kernels: 77.7 us -> 78.6 us
    pallas_call x1 -> x2, Pallas kernels: 77.7 us -> 78.6 us  [the longest x1 77.8 us: body(): pl.pallas_call(functools.partial(kernel, factor), out_shape=shapes, in_sp...]
where the time goes in v5:
time: 79.4 us; the launch traced here: 79.2 us
  Pallas kernels  78.6 us (99%)
    pallas_call x1, Pallas kernels, body(): pl.pallas_call(functools.partial(kernel, factor), out_shape=shapes, in_sp...  77.8 us

profile of v5, /device:TPU:5, one launch (start us, length us, event | category | flops | bytes accessed | tf_op | source)
XLA Modules:
  0.0 79.2 jit_solution(7500447333057880676)
XLA Ops:
  0.6 77.8 %shard_map.101 = (bf16[8,16,768]{2,1,0:T(8,128)(2,1)S(1)}, f32[12,1536]{1,0:T(8,128)S(1)}, f32[12,49]{1,0:T(8,128)S(1)}, f32[1,12]{1,0:T(1,128)S(1)}, f32[1,12]{1,0:T(1,128)S(1)}) custom-call(bf16[8,16,768]{2,1,0:T(8,128)(2,1)} %bitcast.8, bf16[128,1536]{1,0:T(8,128)(2,1)} %bitcast.7, bf16[12,49]{1,0:T(8,128)(2,1)} %dw_hbm.1, bf16[1,12]{1,0:T(2,128)(2,1)} %bitcast.9, ...), custom_call_target="tpu_custom_call" | custom-call | tf_op jit(solution)/shard_map/pallas_call | solution.py:503
  78.5 0.8 shard_map.102
